TPU v7x, 32 devices: a whole 2x2x4 slice. The times are simulated.
32 devices in a mesh: rep: 4 (over y, x), fsdp: 8 (over z, core).
Axes of the slice: x: 2, y: 2, z: 4, core: 2. Of those that a mesh axis runs over, the one named last changes fastest.
Arguments:
- patches: float32 [8192, 1152], P(('rep', 'fsdp')), may hold values from -6 to 6
- cotangent: float32 [8192, 1152], P(('rep', 'fsdp')), may hold values from -6 to 6
- image_ids: int32 [4, 2048], P('rep'), may hold values from 0 to 4, never falling along the last dimension, each value on 1 to 729 neighbouring positions
- input_weight: bfloat16 [2, 1152, 3456], P(None, 'fsdp'), as said below
- output_weight: bfloat16 [2, 1152, 1152], P(None, 'fsdp'), may hold values from -1 to 1
- expand_weight: bfloat16 [2, 1152, 4304], P(None, 'fsdp'), may hold values from -0.1875 to 0.1875
- reduce_weight: bfloat16 [2, 4304, 1152], P(None, 'fsdp'), may hold values from -0.09375 to 0.09375
- first_gain: bfloat16 [2, 1152], P(None, 'fsdp'), may hold values from 0.099609375 to 1.8984375
- first_shift: bfloat16 [2, 1152], P(None, 'fsdp'), may hold values from -3 to 3
- query_bias: bfloat16 [2, 1152], P(None, 'fsdp'), may hold values from -3 to 3
- value_bias: bfloat16 [2, 1152], P(None, 'fsdp'), may hold values from -3 to 3
- output_bias: bfloat16 [2, 1152], P(None, 'fsdp'), may hold values from -3 to 3
- second_gain: bfloat16 [2, 1152], P(None, 'fsdp'), may hold values from 0.099609375 to 1.8984375
- second_shift: bfloat16 [2, 1152], P(None, 'fsdp'), may hold values from -3 to 3
- expand_bias: bfloat16 [2, 4304], P(None, 'fsdp'), may hold values from -3 to 3
- reduce_bias: bfloat16 [2, 1152], P(None, 'fsdp'), may hold values from -3 to 3
Outputs:
- encoded: float32 [8192, 1152], P(('rep', 'fsdp'))
- patch_grad: float32 [8192, 1152], P(('rep', 'fsdp'))
- grad_input_weight: float32 [2, 1152, 3456], P(None, 'fsdp')
- grad_output_weight: float32 [2, 1152, 1152], P(None, 'fsdp')
- grad_expand_weight: float32 [2, 1152, 4304], P(None, 'fsdp')
- grad_reduce_weight: float32 [2, 4304, 1152], P(None, 'fsdp')
- grad_first_gain: float32 [2, 1152], P(None, 'fsdp')
- grad_first_shift: float32 [2, 1152], P(None, 'fsdp')
- grad_query_bias: float32 [2, 1152], P(None, 'fsdp')
- grad_value_bias: float32 [2, 1152], P(None, 'fsdp')
- grad_output_bias: float32 [2, 1152], P(None, 'fsdp')
- grad_second_gain: float32 [2, 1152], P(None, 'fsdp')
- grad_second_shift: float32 [2, 1152], P(None, 'fsdp')
- grad_expand_bias: float32 [2, 4304], P(None, 'fsdp')
- grad_reduce_bias: float32 [2, 1152], P(None, 'fsdp')
Inputs may be any that keep to these rules, and one draw needn't show every extreme that they name: `image_ids`: within each row, one group's 2048 tokens in order, ids never fall and each image holds 1 to 729 consecutive tokens; some image holds exactly 729. `input_weight`: projection weights of fan-in 1152.
All inputs are finite; a program needn't handle non-finite values.
Results may differ from a plain program's by a relative error of at most 0.014.
The roundings to bfloat16 on the way count: a program that leaves them out, or rounds other values in their place, can miss the bound.
Values may be sent and summed in bfloat16 or wider, within the bound.
No kernel may reach another device: no remote copies, remote signals or barrier semaphores. Data moves between devices by JAX's collectives and lax.ppermute only.
A program may use at most 384 MiB of HBM per device.

v0:
```python
from functools import partial
import math

import jax
import jax.numpy as jnp
from jax import lax
from jax.sharding import PartitionSpec as P

D = 1152
HEADS = 16
HEAD_DIM = 72
LAYERS = 2
REACH = 3


EPSILON = 1e-06
GELU_COEF = math.sqrt(2.0 / math.pi)
MASKED = -1e30


def shifted_2(array, axis, by):
    count = lax.axis_size(axis)
    pairs = [(i, i + by) for i in range(count) if 0 <= i + by < count]
    return lax.ppermute(array, axis, pairs)


def norm_forward(values, norm_gain, norm_bias):
    centre = jnp.mean(values, axis=-1, keepdims=True)
    shifted = values - centre
    spread = jnp.mean(shifted * shifted, axis=-1, keepdims=True)
    inverse = lax.rsqrt(spread + EPSILON)
    scaled = shifted * inverse
    return (scaled * norm_gain + norm_bias, scaled, inverse)


def norm_backward(upstream, scaled, inverse, norm_gain):
    weighted = upstream * norm_gain
    mean_one = jnp.mean(weighted, axis=-1, keepdims=True)
    mean_two = jnp.mean(weighted * scaled, axis=-1, keepdims=True)
    result = inverse * (weighted - mean_one - scaled * mean_two)
    return (result, jnp.sum(upstream * scaled, axis=0), jnp.sum(upstream, axis=0))


def gelu_tanh(inputs):
    inside = GELU_COEF * (inputs + 0.044715 * inputs * inputs * inputs)
    return 0.5 * inputs * (1.0 + jnp.tanh(inside))


def gelu_slope(inputs):
    inside = GELU_COEF * (inputs + 0.044715 * inputs * inputs * inputs)
    tangent = jnp.tanh(inside)
    return 0.5 * (1.0 + tangent) + 0.5 * inputs * (1.0 - tangent * tangent) * GELU_COEF * (
        1.0 + 3.0 * 0.044715 * inputs * inputs
    )


def dot_first(left_op, right_op):
    return lax.dot_general(
        left_op, right_op, (((0,), (0,)), ((), ())), preferred_element_type=jnp.float32
    )


def dot_last(left_op, right_op):
    return lax.dot_general(
        left_op, right_op, (((1,), (1,)), ((), ())), preferred_element_type=jnp.float32
    )


def split_heads(matrix):
    return jnp.transpose(matrix.reshape(matrix.shape[0], HEADS, HEAD_DIM), (1, 0, 2))


def join_heads(stacked):
    return jnp.transpose(stacked, (1, 0, 2)).reshape(stacked.shape[1], HEADS * HEAD_DIM)


def head_scores(query_head, key_head, key_mask):
    scores = dot_last(query_head, key_head) * (1.0 / math.sqrt(HEAD_DIM))
    return jnp.where(key_mask, scores, MASKED)


def head_forward(operands, key_mask):
    query_head, key_head, value_head = operands
    scores = head_scores(query_head, key_head, key_mask)
    highest = jnp.max(scores, axis=-1, keepdims=True)
    log_sum = highest + jnp.log(jnp.sum(jnp.exp(scores - highest), axis=-1, keepdims=True))
    weights_low = jnp.exp(scores - log_sum).astype(jnp.bfloat16)
    return (jnp.dot(weights_low, value_head, preferred_element_type=jnp.float32), log_sum[:, 0])


def head_backward(operands, key_mask):
    query_head, key_head, value_head, grad_head, attended_head, log_sum = operands
    scores = head_scores(query_head, key_head, key_mask)
    probabilities = jnp.exp(scores - log_sum[:, None])
    grad_probs = dot_last(grad_head, value_head)
    row_dot = jnp.sum(grad_head.astype(jnp.float32) * attended_head, axis=-1, keepdims=True)
    grad_scores = (probabilities * (grad_probs - row_dot) * (1.0 / math.sqrt(HEAD_DIM))).astype(
        jnp.bfloat16
    )
    grad_query = jnp.dot(grad_scores, key_head, preferred_element_type=jnp.float32)
    grad_keys = dot_first(grad_scores, query_head)
    grad_values = dot_first(probabilities.astype(jnp.bfloat16), grad_head)
    return (grad_query, grad_keys, grad_values)


def fetch_before(key_block, value_block, offset):
    return shifted_2((key_block, value_block), "fsdp", offset)


def fetch_after(key_block, value_block, offset):
    return shifted_2((key_block, value_block), "fsdp", -offset)


def return_before(key_grad, value_grad, offset):
    return shifted_2((key_grad, value_grad), "fsdp", -offset)


def return_after(key_grad, value_grad, offset):
    return shifted_2((key_grad, value_grad), "fsdp", offset)


def body(
    patches,
    cotangent,
    image_ids,
    input_weight,
    output_weight,
    expand_weight,
    reduce_weight,
    first_gain,
    first_shift,
    query_bias,
    value_bias,
    output_bias,
    second_gain,
    second_shift,
    expand_bias,
    reduce_bias,
):
    span_len = patches.shape[0]
    position = lax.axis_index("fsdp")
    ids_row = image_ids[0]
    padding = jnp.full((REACH * span_len,), -1, jnp.int32)
    padded = jnp.concatenate([padding, ids_row, padding])
    key_ids = lax.dynamic_slice_in_dim(padded, position * span_len, (2 * REACH + 1) * span_len)
    query_ids = lax.dynamic_slice_in_dim(ids_row, position * span_len, span_len)
    key_mask = query_ids[:, None] == key_ids[None, :]
    stored_layers = []
    stream = patches
    for layer_index in range(LAYERS):
        attention_set = (
            lax.all_gather(input_weight[layer_index], "fsdp", axis=0, tiled=True),
            lax.all_gather(output_weight[layer_index], "fsdp", axis=0, tiled=True),
            lax.all_gather(first_gain[layer_index], "fsdp", axis=0, tiled=True),
            lax.all_gather(first_shift[layer_index], "fsdp", axis=0, tiled=True),
            lax.all_gather(query_bias[layer_index], "fsdp", axis=0, tiled=True),
            lax.all_gather(value_bias[layer_index], "fsdp", axis=0, tiled=True),
            lax.all_gather(output_bias[layer_index], "fsdp", axis=0, tiled=True),
        )
        input_matrix, output_matrix, gain_one, shift_one, bias_query, bias_value, bias_output = (
            attention_set
        )
        normed, scaled_one, inverse_one = norm_forward(
            stream, gain_one.astype(jnp.float32), shift_one.astype(jnp.float32)
        )
        normed_low = normed.astype(jnp.bfloat16)
        projected = jnp.dot(normed_low, input_matrix, preferred_element_type=jnp.float32)
        queries = (projected[:, :D] + bias_query.astype(jnp.float32)).astype(jnp.bfloat16)
        key_rows = projected[:, D : 2 * D].astype(jnp.bfloat16)
        value_rows = (projected[:, 2 * D :] + bias_value.astype(jnp.float32)).astype(jnp.bfloat16)
        key_parts = []
        value_parts = []
        for offset in range(REACH, 0, -1):
            far_keys, far_values = fetch_before(key_rows, value_rows, offset)
            key_parts.append(far_keys)
            value_parts.append(far_values)
        key_parts.append(key_rows)
        value_parts.append(value_rows)
        for offset in range(1, REACH + 1):
            far_keys, far_values = fetch_after(key_rows, value_rows, offset)
            key_parts.append(far_keys)
            value_parts.append(far_values)
        all_keys = jnp.concatenate(key_parts, axis=0)
        all_values = jnp.concatenate(value_parts, axis=0)
        head_out, log_sums = lax.map(
            partial(head_forward, key_mask=key_mask),
            (split_heads(queries), split_heads(all_keys), split_heads(all_values)),
        )
        attended = join_heads(head_out)
        attended_low = attended.astype(jnp.bfloat16)
        middle = (
            stream
            + jnp.dot(attended_low, output_matrix, preferred_element_type=jnp.float32)
            + bias_output.astype(jnp.float32)
        )
        feed_set = (
            lax.all_gather(expand_weight[layer_index], "fsdp", axis=0, tiled=True),
            lax.all_gather(reduce_weight[layer_index], "fsdp", axis=0, tiled=True),
            lax.all_gather(second_gain[layer_index], "fsdp", axis=0, tiled=True),
            lax.all_gather(second_shift[layer_index], "fsdp", axis=0, tiled=True),
            lax.all_gather(expand_bias[layer_index], "fsdp", axis=0, tiled=True),
            lax.all_gather(reduce_bias[layer_index], "fsdp", axis=0, tiled=True),
        )
        expand_matrix, reduce_matrix, gain_two, shift_two, bias_expand, bias_reduce = feed_set
        normed_two, scaled_two, inverse_two = norm_forward(
            middle, gain_two.astype(jnp.float32), shift_two.astype(jnp.float32)
        )
        normed_two = normed_two.astype(jnp.bfloat16)
        hidden_pre = jnp.dot(
            normed_two, expand_matrix, preferred_element_type=jnp.float32
        ) + bias_expand.astype(jnp.float32)
        hidden_low = gelu_tanh(hidden_pre).astype(jnp.bfloat16)
        stream = (
            middle
            + jnp.dot(hidden_low, reduce_matrix, preferred_element_type=jnp.float32)
            + bias_reduce.astype(jnp.float32)
        )
        stored_layers.append(
            (
                attention_set,
                feed_set,
                scaled_one,
                inverse_one,
                normed_low,
                queries,
                all_keys,
                all_values,
                attended,
                log_sums,
                attended_low,
                scaled_two,
                inverse_two,
                normed_two,
                hidden_pre,
                hidden_low,
            )
        )
    upstream = cotangent
    layer_grads = [None] * LAYERS
    for layer_index in range(LAYERS - 1, -1, -1):
        (
            attention_set,
            feed_set,
            scaled_one,
            inverse_one,
            normed_low,
            queries,
            all_keys,
            all_values,
            attended,
            log_sums,
            attended_low,
            scaled_two,
            inverse_two,
            normed_two,
            hidden_pre,
            hidden_low,
        ) = stored_layers[layer_index]
        attention_set = (
            lax.all_gather(input_weight[layer_index], "fsdp", axis=0, tiled=True),
            lax.all_gather(output_weight[layer_index], "fsdp", axis=0, tiled=True),
            lax.all_gather(first_gain[layer_index], "fsdp", axis=0, tiled=True),
            lax.all_gather(first_shift[layer_index], "fsdp", axis=0, tiled=True),
            lax.all_gather(query_bias[layer_index], "fsdp", axis=0, tiled=True),
            lax.all_gather(value_bias[layer_index], "fsdp", axis=0, tiled=True),
            lax.all_gather(output_bias[layer_index], "fsdp", axis=0, tiled=True),
        )
        feed_set = (
            lax.all_gather(expand_weight[layer_index], "fsdp", axis=0, tiled=True),
            lax.all_gather(reduce_weight[layer_index], "fsdp", axis=0, tiled=True),
            lax.all_gather(second_gain[layer_index], "fsdp", axis=0, tiled=True),
            lax.all_gather(second_shift[layer_index], "fsdp", axis=0, tiled=True),
            lax.all_gather(expand_bias[layer_index], "fsdp", axis=0, tiled=True),
            lax.all_gather(reduce_bias[layer_index], "fsdp", axis=0, tiled=True),
        )
        input_matrix, output_matrix, gain_one, shift_one, bias_query, bias_value, bias_output = (
            attention_set
        )
        expand_matrix, reduce_matrix, gain_two, shift_two, bias_expand, bias_reduce = feed_set
        upstream_low = upstream.astype(jnp.bfloat16)
        grad_reduce = dot_first(hidden_low, upstream_low)
        grad_reduce_bias = jnp.sum(upstream, axis=0)
        grad_pre = dot_last(upstream_low, reduce_matrix) * gelu_slope(hidden_pre)
        grad_pre_low = grad_pre.astype(jnp.bfloat16)
        grad_expand = dot_first(normed_two, grad_pre_low)
        grad_expand_bias = jnp.sum(grad_pre, axis=0)
        grad_normed_two = dot_last(grad_pre_low, expand_matrix)
        part_two, grad_gain_two, grad_shift_two = norm_backward(
            grad_normed_two, scaled_two, inverse_two, gain_two.astype(jnp.float32)
        )
        grad_middle = upstream + part_two
        grad_middle_low = grad_middle.astype(jnp.bfloat16)
        grad_output = dot_first(attended_low, grad_middle_low)
        grad_output_bias = jnp.sum(grad_middle, axis=0)
        grad_attended = dot_last(grad_middle_low, output_matrix).astype(jnp.bfloat16)
        grad_query_heads, grad_key_heads, grad_value_heads = lax.map(
            partial(head_backward, key_mask=key_mask),
            (
                split_heads(queries),
                split_heads(all_keys),
                split_heads(all_values),
                split_heads(grad_attended),
                split_heads(attended),
                log_sums,
            ),
        )
        grad_queries = join_heads(grad_query_heads)
        grad_keys_all = join_heads(grad_key_heads)
        grad_values_all = join_heads(grad_value_heads)
        key_grad = grad_keys_all[REACH * span_len : (REACH + 1) * span_len]
        value_grad = grad_values_all[REACH * span_len : (REACH + 1) * span_len]
        for offset in range(1, REACH + 1):
            start_before = (REACH - offset) * span_len
            back_keys, back_values = return_before(
                grad_keys_all[start_before : start_before + span_len],
                grad_values_all[start_before : start_before + span_len],
                offset,
            )
            key_grad = key_grad + back_keys
            value_grad = value_grad + back_values
            start_after = (REACH + offset) * span_len
            back_keys, back_values = return_after(
                grad_keys_all[start_after : start_after + span_len],
                grad_values_all[start_after : start_after + span_len],
                offset,
            )
            key_grad = key_grad + back_keys
            value_grad = value_grad + back_values
        grad_projected = jnp.concatenate([grad_queries, key_grad, value_grad], axis=1).astype(
            jnp.bfloat16
        )
        grad_input = dot_first(normed_low, grad_projected)
        grad_query_bias = jnp.sum(grad_queries, axis=0)
        grad_value_bias = jnp.sum(value_grad, axis=0)
        grad_normed = dot_last(grad_projected, input_matrix)
        part_one, grad_gain_one, grad_shift_one = norm_backward(
            grad_normed, scaled_one, inverse_one, gain_one.astype(jnp.float32)
        )
        upstream = grad_middle + part_one
        (
            share_input,
            share_output,
            share_gain_one,
            share_shift_one,
            share_query,
            share_value,
            share_out_bias,
        ) = (
            lax.psum_scatter(grad_input, "fsdp", scatter_dimension=0, tiled=True),
            lax.psum_scatter(grad_output, "fsdp", scatter_dimension=0, tiled=True),
            lax.psum_scatter(grad_gain_one, "fsdp", scatter_dimension=0, tiled=True),
            lax.psum_scatter(grad_shift_one, "fsdp", scatter_dimension=0, tiled=True),
            lax.psum_scatter(grad_query_bias, "fsdp", scatter_dimension=0, tiled=True),
            lax.psum_scatter(grad_value_bias, "fsdp", scatter_dimension=0, tiled=True),
            lax.psum_scatter(grad_output_bias, "fsdp", scatter_dimension=0, tiled=True),
        )
        (
            share_expand,
            share_reduce,
            share_gain_two,
            share_shift_two,
            share_expand_bias,
            share_reduce_bias,
        ) = (
            lax.psum_scatter(grad_expand, "fsdp", scatter_dimension=0, tiled=True),
            lax.psum_scatter(grad_reduce, "fsdp", scatter_dimension=0, tiled=True),
            lax.psum_scatter(grad_gain_two, "fsdp", scatter_dimension=0, tiled=True),
            lax.psum_scatter(grad_shift_two, "fsdp", scatter_dimension=0, tiled=True),
            lax.psum_scatter(grad_expand_bias, "fsdp", scatter_dimension=0, tiled=True),
            lax.psum_scatter(grad_reduce_bias, "fsdp", scatter_dimension=0, tiled=True),
        )
        layer_grads[layer_index] = lax.psum(
            (
                share_input,
                share_output,
                share_expand,
                share_reduce,
                share_gain_one,
                share_shift_one,
                share_query,
                share_value,
                share_out_bias,
                share_gain_two,
                share_shift_two,
                share_expand_bias,
                share_reduce_bias,
            ),
            "rep",
        )
    stacked = [
        jnp.stack([layer_grads[layer_index][member] for layer_index in range(LAYERS)])
        for member in range(13)
    ]
    return (
        stream,
        upstream,
        stacked[0],
        stacked[1],
        stacked[2],
        stacked[3],
        stacked[4],
        stacked[5],
        stacked[6],
        stacked[7],
        stacked[8],
        stacked[9],
        stacked[10],
        stacked[11],
        stacked[12],
    )


def solution(mesh):
    placed = (
        P(("rep", "fsdp"), None),
        P(("rep", "fsdp"), None),
        P("rep", None),
        P(None, "fsdp", None),
        P(None, "fsdp", None),
        P(None, "fsdp", None),
        P(None, "fsdp", None),
        P(None, "fsdp"),
        P(None, "fsdp"),
        P(None, "fsdp"),
        P(None, "fsdp"),
        P(None, "fsdp"),
        P(None, "fsdp"),
        P(None, "fsdp"),
        P(None, "fsdp"),
        P(None, "fsdp"),
    )
    return jax.shard_map(
        body,
        mesh=mesh,
        in_specs=placed,
        out_specs=(
            P(("rep", "fsdp"), None),
            P(("rep", "fsdp"), None),
            P(None, "fsdp", None),
            P(None, "fsdp", None),
            P(None, "fsdp", None),
            P(None, "fsdp", None),
            P(None, "fsdp"),
            P(None, "fsdp"),
            P(None, "fsdp"),
            P(None, "fsdp"),
            P(None, "fsdp"),
            P(None, "fsdp"),
            P(None, "fsdp"),
            P(None, "fsdp"),
            P(None, "fsdp"),
        ),
        check_vma=False,
    )
```

profile of v0, /device:TPU:0, one launch (start us, length us, event | category | flops | bytes accessed | tf_op | source)
XLA Modules:
  0.0 3021.8 jit_solution(2510062662433458572)
XLA Ops:
  28.2 35.3 %all-reduce.43 = (bf16[1152]{0:T(1024)(128)(2,1)S(1)}, bf16[1152]{0:T(1024)(128)(2,1)S(1)}, bf16[1152]{0:T(1024)(128)(2,1)S(1)}, bf16[1152]{0:T(1024)(128)(2,1)S...) all-reduce(bf16[1152]{0:T(1024)(128)(2,1)S(1)} %dynamic-update-slic, ...), channel_id=3, replica_groups=mesh['rep'=4,'fsdp'=8] {'fsdp'}, use_global_device_ids=true, to_apply=%add.1 | all-reduce | flops 27040 | bytes 108160
  64.7 28.5 all-gather.35.cloned.1.call-done
  128.6 16.3 collective-permute-start.6
  175.6 15.8 collective-permute-done.7
  201.7 60.0 %collective-permute-done.5 = bf16[256,1152]{1,0:T(8,128)(2,1)S(1)} collective-permute-done((bf16[256,1152]{1,0:T(8,128)(2,1)S(1)}, bf16[256,1152]{1,0:T(8,128)(2,1)S(1)}, u32[]{:S(2)}, u32[]{:S(2)}) %collective-permute-start.5) | collective-permute-done | bytes 589856 | tf_op jit(solution)/shard_map/ppermute | solution.py:24
  279.9 26.8 collective-permute-done.11
  323.3 57.9 %while.56 = (s32[]{:T(128)}, f32[16,256,72]{1,2,0:T(8,128)S(1)}, f32[16,256]{1,0:T(8,128)S(1)}, bf16[16,256,72]{2,1,0:T(8,128)(2,1)}, bf16[16,1792,72]{2,1,0:T(8...) while((s32[]{:T(128)}, f32[16,256,72]{1,2,0:T(8,128)S(1)}, ...), condition=%wide.region_5.6_spmd.clone, body=%wide.region_2.5_spmd.clone.sunk | while | flops 135790336 | bytes 6581361 | solution.py:185
  396.1 81.9 %all-gather.41.cloned.1.call-done = bf16[1,4304,1152]{2,0,1:T(2,128)(2,1)} async-done(((bf16[1,538,1152]{2,0,1:T(2,128)(2,1)}), bf16[1,4304,1152]{2,0,1:T(2,128)(2,1)}) %all-gather.41.cloned.1.call-update) | async-done | bytes 9916432 | tf_op jit(solution)/shard_map/all_gather | solution.py:198
  489.8 67.1 %all-gather.43.cloned.1.call-done = bf16[1,1152,3456]{2,1,0:T(8,128)(2,1)} async-done(((bf16[1,144,3456]{2,1,0:T(8,128)(2,1)}), bf16[1,1152,3456]{2,1,0:T(8,128)(2,1)}) %all-gather.43.cloned.1.call-update) | async-done | bytes 7962640 | tf_op jit(solution)/shard_map/all_gather | solution.py:152
  592.7 15.9 collective-permute-start.18
  639.1 15.7 collective-permute-done.19
  665.2 60.4 %collective-permute-done.17 = bf16[256,1152]{1,0:T(8,128)(2,1)S(1)} collective-permute-done((bf16[256,1152]{1,0:T(8,128)(2,1)}, bf16[256,1152]{1,0:T(8,128)(2,1)S(1)}, u32[]{:S(2)}, u32[]{:S(2)}) %collective-permute-start.17) | collective-permute-done | bytes 589856 | tf_op jit(solution)/shard_map/ppermute | solution.py:24
  733.2 36.6 %collective-permute-done.23 = bf16[256,1152]{1,0:T(8,128)(2,1)S(1)} collective-permute-done((bf16[256,1152]{1,0:T(8,128)(2,1)S(1)}, bf16[256,1152]{1,0:T(8,128)(2,1)S(1)}, u32[]{:S(2)}, u32[]{:S(2)}) %collective-permute-start.23) | collective-permute-done | bytes 589856 | tf_op jit(solution)/shard_map/ppermute | solution.py:24
  799.6 57.8 %while.57 = (s32[]{:T(128)}, f32[16,256,72]{1,2,0:T(8,128)S(1)}, f32[16,256]{1,0:T(8,128)S(1)}, bf16[16,256,72]{2,1,0:T(8,128)(2,1)}, bf16[16,1792,72]{2,1,0:T(8...) while((s32[]{:T(128)}, f32[16,256,72]{1,2,0:T(8,128)S(1)}, ...), condition=%wide.region_13.14_spmd.clone, body=%wide.region_10.13_spmd.clone.sunk | while | flops 135790336 | bytes 6581361 | solution.py:185
  872.6 68.8 %all-gather.49.cloned.1.call-done = bf16[1,4304,1152]{2,0,1:T(2,128)(2,1)} async-done(((bf16[1,538,1152]{2,0,1:T(2,128)(2,1)}), bf16[1,4304,1152]{2,0,1:T(2,128)(2,1)}) %all-gather.49.cloned.1.call-update) | async-done | bytes 9916432 | tf_op jit(solution)/shard_map/all_gather | solution.py:198
  941.4 13.2 fusion.235
  982.1 177.4 %while.58 = (s32[]{:T(128)}, f32[16,256,72]{1,2,0:T(8,128)}, f32[16,1792,72]{1,2,0:T(8,128)}, f32[16,1792,72]{1,2,0:T(8,128)}, bf16[16,256,72]{2,1,0:T(8,128)(2,...) while((s32[]{:T(128)}, f32[16,256,72]{1,2,0:T(8,128)}, ...), condition=%wide.region_20.21_spmd.clone, body=%wide.region_18.20_spmd.clone.sunk | while | flops 334485248 | bytes 11516049 | solution.py:296
  1179.2 15.5 collective-permute-done.35
  1221.3 19.3 collective-permute-start.27
  1253.1 17.4 collective-permute-done.27
  1343.0 188.5 %while.59 = (s32[]{:T(128)}, f32[16,256,72]{1,2,0:T(8,128)}, f32[16,1792,72]{1,2,0:T(8,128)}, f32[16,1792,72]{1,2,0:T(8,128)}, bf16[16,256,72]{2,1,0:T(8,128)(2,...) while((s32[]{:T(128)}, f32[16,256,72]{1,2,0:T(8,128)}, ...), condition=%wide.region_27.28_spmd.clone, body=%wide.region_25.27_spmd.clone.sunk | while | flops 334485248 | bytes 11516049 | solution.py:296
  1538.2 37.4 %collective-permute-start.47 = (f32[256,1152]{0,1:T(8,128)}, f32[256,1152]{0,1:T(8,128)S(1)}, u32[]{:S(2)}, u32[]{:S(2)}) collective-permute-start(f32[256,1152]{0,1:T(8,128)} %bitcast.71), channel_id=1, source_target_pairs={{0,3},{1,4},{2,5},{3,6},{4,7},{8,11},{9,12},{10,13},{11,14},{12,15... | collective-permute-start | bytes 3538952 | tf_op jit(solution)/shard_map/ppermute | solution.py:24
  1586.8 15.4 collective-permute-done.47
  1639.4 15.2 collective-permute-start.37
  1658.7 19.3 collective-permute-done.39
  1703.4 13.3 fusion.205
  1725.3 432.8 %fusion.9 = f32[544,1152]{1,0:T(8,128)} fusion(f32[4304,1152]{1,0:T(8,128)} %fusion.205), kind=kCustom, calls=%all-reduce-scatter.1 | all-reduce-scatter fusion | flops 5013505 | bytes 22340096
  2183.8 404.6 %fusion.8 = f32[544,1152]{1,0:T(8,128)} fusion(f32[4304,1152]{1,0:T(8,128)} %fusion.199), kind=kCustom, calls=%all-reduce-scatter | all-reduce-scatter fusion | flops 5013505 | bytes 22340096
  2616.3 29.1 reduce-scatter.19.cloned.1.call-done
  2661.2 45.5 %all-reduce.47.cloned.1.call-done = (f32[1152]{0:T(1024)}, f32[1152]{0:T(1024)}, f32[1152]{0:T(1024)}, f32[1152]{0:T(1024)}, f32[1152]{0:T(1024)}, /*index=5*/f3...) async-done(((f32[1152]{0:T(1024)}, f32[1152]{0:T(1024)}, ...) | async-done | bytes 108176
  2720.6 18.0 all-reduce.41
  2743.9 254.7 %all-reduce.49.cloned.1.call-done = (f32[1,144,3456]{2,1,0:T(8,128)}, f32[1,144,3456]{2,1,0:T(8,128)}, f32[1,144,1152]{2,1,0:T(8,128)}, f32[1,144,1152]{2,1,0:T(...) async-done(((f32[1,144,3456]{2,1,0:T(8,128)}, f32[1,144,3456]{2,1,0:T(8,128)}, ...) | async-done | bytes 15224848 | tf_op jit(solution)/shard_map/psum | solution.py:372
  (1056 shorter events, 1120.5 us)
Async XLA Ops:
  7.2 86.1 %all-gather.35.cloned.1.call-start = ((), (), s32[]{:S(2)}) async-start(), calls=%async_computation.12 | async-start | bytes 8957952 | tf_op jit(solution)/shard_map/all_gather | solution.py:152
  10.2 371.1 %all-gather.37.cloned.1.call-start = ((), (), s32[]{:S(2)}) async-start(), calls=%async_computation.13 | async-start | bytes 2985984 | tf_op jit(solution)/shard_map/all_gather | solution.py:153
  11.2 374.3 %all-gather.39.cloned.1.call-start = ((), (), s32[]{:S(2)}) async-start(), calls=%async_computation.14 | async-start | bytes 11280384 | tf_op jit(solution)/shard_map/all_gather | solution.py:197
  14.7 463.2 %all-gather.41.cloned.1.call-start = ((), (), s32[]{:S(2)}) async-start(), calls=%async_computation.15 | async-start | bytes 22311936 | tf_op jit(solution)/shard_map/all_gather | solution.py:198
  19.9 537.0 %all-gather.43.cloned.1.call-start = ((), (), s32[]{:S(2)}) async-start(), calls=%async_computation.16 | async-start | bytes 8957952 | tf_op jit(solution)/shard_map/all_gather | solution.py:152
  20.5 837.0 %all-gather.45.cloned.1.call-start = ((), (), s32[]{:S(2)}) async-start(), calls=%async_computation.17 | async-start | bytes 2985984 | tf_op jit(solution)/shard_map/all_gather | solution.py:153
  21.1 840.8 %all-gather.47.cloned.1.call-start = ((), (), s32[]{:S(2)}) async-start(), calls=%async_computation.18 | async-start | bytes 11280384 | tf_op jit(solution)/shard_map/all_gather | solution.py:197
  21.9 919.6 %all-gather.49.cloned.1.call-start = ((), (), s32[]{:S(2)}) async-start(), calls=%async_computation.19 | async-start | bytes 22311936 | tf_op jit(solution)/shard_map/all_gather | solution.py:198
  113.8 82.8 %collective-permute-start.3 = (bf16[256,1152]{1,0:T(8,128)(2,1)S(1)}, bf16[256,1152]{1,0:T(8,128)(2,1)}, u32[]{:S(2)}, u32[]{:S(2)}) collective-permute-start(bf16[256,1152]{1,0:T(8,128)(2,1)S(1)} %slice.435), channel_id=1, source_target_pairs={{1,0},{2,1},{3,2},{4,3},{5,4},{6,5},{7,6},{9,8},{10,9},{11,10},{12... | collective-permute-start | bytes 1769480 | tf_op jit(solution)/shard_map/ppermute | solution.py:24
  115.1 84.8 %collective-permute-start.4 = (bf16[256,1152]{1,0:T(8,128)(2,1)S(1)}, bf16[256,1152]{1,0:T(8,128)(2,1)}, u32[]{:S(2)}, u32[]{:S(2)}) collective-permute-start(bf16[256,1152]{1,0:T(8,128)(2,1)S(1)} %slice.435), channel_id=1, source_target_pairs={{2,0},{3,1},{4,2},{5,3},{6,4},{7,5},{10,8},{11,9},{12,10},{13,11},... | collective-permute-start | bytes 1769480 | tf_op jit(solution)/shard_map/ppermute | solution.py:24
  173.5 88.2 %collective-permute-start.5 = (bf16[256,1152]{1,0:T(8,128)(2,1)S(1)}, bf16[256,1152]{1,0:T(8,128)(2,1)S(1)}, u32[]{:S(2)}, u32[]{:S(2)}) collective-permute-start(bf16[256,1152]{1,0:T(8,128)(2,1)S(1)} %slice.435), channel_id=1, source_target_pairs={{3,0},{4,1},{5,2},{6,3},{7,4},{11,8},{12,9},{13,10},{14,11},{15,12... | collective-permute-start | bytes 1769480 | tf_op jit(solution)/shard_map/ppermute | solution.py:24
  191.4 85.7 %collective-permute-start.9 = (bf16[256,1152]{1,0:T(8,128)(2,1)S(1)}, bf16[256,1152]{1,0:T(8,128)(2,1)S(1)}, u32[]{:S(2)}, u32[]{:S(2)}) collective-permute-start(bf16[256,1152]{1,0:T(8,128)(2,1)S(1)} %get-tuple-element.684), channel_id=1, source_target_pairs={{1,0},{2,1},{3,2},{4,3},{5,4},{6,5},{7,6},{9,8},{10,9},{11,10},{12... | collective-permute-start | bytes 1769480 | tf_op jit(solution)/shard_map/ppermute | solution.py:24
  193.5 84.4 %collective-permute-start.10 = (bf16[256,1152]{1,0:T(8,128)(2,1)S(1)}, bf16[256,1152]{1,0:T(8,128)(2,1)}, u32[]{:S(2)}, u32[]{:S(2)}) collective-permute-start(bf16[256,1152]{1,0:T(8,128)(2,1)S(1)} %get-tuple-element.684), channel_id=1, source_target_pairs={{2,0},{3,1},{4,2},{5,3},{6,4},{7,5},{10,8},{11,9},{12,10},{13,11},... | collective-permute-start | bytes 1769480 | tf_op jit(solution)/shard_map/ppermute | solution.py:24
  196.6 110.1 %collective-permute-start.11 = (bf16[256,1152]{1,0:T(8,128)(2,1)S(1)}, bf16[256,1152]{1,0:T(8,128)(2,1)}, u32[]{:S(2)}, u32[]{:S(2)}) collective-permute-start(bf16[256,1152]{1,0:T(8,128)(2,1)S(1)} %get-tuple-element.684), channel_id=1, source_target_pairs={{3,0},{4,1},{5,2},{6,3},{7,4},{11,8},{12,9},{13,10},{14,11},{15,12... | collective-permute-start | bytes 1769480 | tf_op jit(solution)/shard_map/ppermute | solution.py:24
  567.2 2049.1 %reduce-scatter.17.cloned.1.call-start = ((), (), s32[]{:S(2)}) async-start(), calls=%async_computation.9 | async-start | bytes 5971968 | tf_op jit(solution)/shard_map/reduce_scatter | solution.py:350
  572.1 51.4 %collective-permute-start.14 = (bf16[256,1152]{1,0:T(8,128)(2,1)}, bf16[256,1152]{1,0:T(8,128)(2,1)}, u32[]{:S(2)}, u32[]{:S(2)}) collective-permute-start(bf16[256,1152]{1,0:T(8,128)(2,1)} %slice.434), channel_id=1, source_target_pairs={{0,1},{1,2},{2,3},{3,4},{4,5},{5,6},{6,7},{8,9},{9,10},{10,11},{11... | collective-permute-start | bytes 1769480 | tf_op jit(solution)/shard_map/ppermute | solution.py:24
  574.2 85.8 %collective-permute-start.15 = (bf16[256,1152]{1,0:T(8,128)(2,1)}, bf16[256,1152]{1,0:T(8,128)(2,1)}, u32[]{:S(2)}, u32[]{:S(2)}) collective-permute-start(bf16[256,1152]{1,0:T(8,128)(2,1)} %slice.434), channel_id=1, source_target_pairs={{1,0},{2,1},{3,2},{4,3},{5,4},{6,5},{7,6},{9,8},{10,9},{11,10},{12... | collective-permute-start | bytes 1769480 | tf_op jit(solution)/shard_map/ppermute | solution.py:24
  575.5 87.7 %collective-permute-start.16 = (bf16[256,1152]{1,0:T(8,128)(2,1)}, bf16[256,1152]{1,0:T(8,128)(2,1)}, u32[]{:S(2)}, u32[]{:S(2)}) collective-permute-start(bf16[256,1152]{1,0:T(8,128)(2,1)} %slice.434), channel_id=1, source_target_pairs={{2,0},{3,1},{4,2},{5,3},{6,4},{7,5},{10,8},{11,9},{12,10},{13,11},... | collective-permute-start | bytes 1769480 | tf_op jit(solution)/shard_map/ppermute | solution.py:24
  636.9 88.6 %collective-permute-start.17 = (bf16[256,1152]{1,0:T(8,128)(2,1)}, bf16[256,1152]{1,0:T(8,128)(2,1)S(1)}, u32[]{:S(2)}, u32[]{:S(2)}) collective-permute-start(bf16[256,1152]{1,0:T(8,128)(2,1)} %slice.434), channel_id=1, source_target_pairs={{3,0},{4,1},{5,2},{6,3},{7,4},{11,8},{12,9},{13,10},{14,11},{15,12... | collective-permute-start | bytes 1769480 | tf_op jit(solution)/shard_map/ppermute | solution.py:24
  654.8 71.6 %collective-permute-start.21 = (bf16[256,1152]{1,0:T(8,128)(2,1)S(1)}, bf16[256,1152]{1,0:T(8,128)(2,1)S(1)}, u32[]{:S(2)}, u32[]{:S(2)}) collective-permute-start(bf16[256,1152]{1,0:T(8,128)(2,1)S(1)} %get-tuple-element.682), channel_id=1, source_target_pairs={{1,0},{2,1},{3,2},{4,3},{5,4},{6,5},{7,6},{9,8},{10,9},{11,10},{12... | collective-permute-start | bytes 1769480 | tf_op jit(solution)/shard_map/ppermute | solution.py:24
  657.0 75.3 %collective-permute-start.22 = (bf16[256,1152]{1,0:T(8,128)(2,1)S(1)}, bf16[256,1152]{1,0:T(8,128)(2,1)S(1)}, u32[]{:S(2)}, u32[]{:S(2)}) collective-permute-start(bf16[256,1152]{1,0:T(8,128)(2,1)S(1)} %get-tuple-element.682), channel_id=1, source_target_pairs={{2,0},{3,1},{4,2},{5,3},{6,4},{7,5},{10,8},{11,9},{12,10},{13,11},... | collective-permute-start | bytes 1769480 | tf_op jit(solution)/shard_map/ppermute | solution.py:24
  660.0 109.7 %collective-permute-start.23 = (bf16[256,1152]{1,0:T(8,128)(2,1)S(1)}, bf16[256,1152]{1,0:T(8,128)(2,1)S(1)}, u32[]{:S(2)}, u32[]{:S(2)}) collective-permute-start(bf16[256,1152]{1,0:T(8,128)(2,1)S(1)} %get-tuple-element.682), channel_id=1, source_target_pairs={{3,0},{4,1},{5,2},{6,3},{7,4},{11,8},{12,9},{13,10},{14,11},{15,12... | collective-permute-start | bytes 1769480 | tf_op jit(solution)/shard_map/ppermute | solution.py:24
  973.1 1643.2 %reduce-scatter.15.cloned.1.call-start = ((), (), s32[]{:S(2)}) async-start(), calls=%async_computation.8 | async-start | bytes 5971968 | tf_op jit(solution)/shard_map/reduce_scatter | solution.py:350
  1172.1 68.5 %collective-permute-start.31 = (f32[256,1152]{0,1:T(8,128)}, f32[256,1152]{0,1:T(8,128)S(1)}, u32[]{:S(2)}, u32[]{:S(2)}) collective-permute-start(f32[256,1152]{0,1:T(8,128)} %bitcast.44), channel_id=1, source_target_pairs={{0,1},{1,2},{2,3},{3,4},{4,5},{5,6},{6,7},{8,9},{9,10},{10,11},{11... | collective-permute-start | bytes 3538952 | tf_op jit(solution)/shard_map/ppermute | solution.py:24
  1318.3 1298.0 %reduce-scatter.13.cloned.1.call-start = ((), (), s32[]{:S(2)}) async-start(), calls=%async_computation.7 | async-start | bytes 17915904 | tf_op jit(solution)/shard_map/reduce_scatter | solution.py:349
  1334.0 1282.3 %reduce-scatter.11.cloned.1.call-start = ((), (), s32[]{:S(2)}) async-start(), calls=%async_computation.6 | async-start | bytes 17915904 | tf_op jit(solution)/shard_map/reduce_scatter | solution.py:349
  1538.2 64.0 %collective-permute-start.47 = (f32[256,1152]{0,1:T(8,128)}, f32[256,1152]{0,1:T(8,128)S(1)}, u32[]{:S(2)}, u32[]{:S(2)}) collective-permute-start(f32[256,1152]{0,1:T(8,128)} %bitcast.71), channel_id=1, source_target_pairs={{0,3},{1,4},{2,5},{3,6},{4,7},{8,11},{9,12},{10,13},{11,14},{12,15... | collective-permute-start | bytes 3538952 | tf_op jit(solution)/shard_map/ppermute | solution.py:24
  1579.6 58.5 %collective-permute-start.43 = (f32[256,1152]{0,1:T(8,128)}, f32[256,1152]{0,1:T(8,128)S(1)}, u32[]{:S(2)}, u32[]{:S(2)}) collective-permute-start(f32[256,1152]{0,1:T(8,128)} %bitcast.67), channel_id=1, source_target_pairs={{0,1},{1,2},{2,3},{3,4},{4,5},{5,6},{6,7},{8,9},{9,10},{10,11},{11... | collective-permute-start | bytes 3538952 | tf_op jit(solution)/shard_map/ppermute | solution.py:24
  1690.4 925.9 %reduce-scatter.21.cloned.1.call-start = ((), (), s32[]{:S(2)}) async-start(), calls=%async_computation.11 | async-start | bytes 22560768 | tf_op jit(solution)/shard_map/reduce_scatter | solution.py:365
  1702.9 942.5 %reduce-scatter.19.cloned.1.call-start = ((), (), s32[]{:S(2)}) async-start(), calls=%async_computation.10 | async-start | bytes 22560768 | tf_op jit(solution)/shard_map/reduce_scatter | solution.py:365
  1725.3 981.5 %all-reduce.47.cloned.1.call-start = ((), (), s32[]{:S(2)}) async-start(), calls=%async_computation.20 | async-start | bytes 344064
  2612.8 385.8 %all-reduce.49.cloned.1.call-start = ((), (), s32[]{:S(2)}) async-start(), calls=%async_computation.21 | async-start | bytes 30670848 | tf_op jit(solution)/shard_map/psum | solution.py:372
  (127 other events, 3511.3 us)
Sparse Core Ops, SparseCore 0:
  10.4 82.8 all-gather.34
  94.9 47.3 all-gather.36
  143.9 123.1 all-gather.38
  268.6 209.3 all-gather.40
  480.0 76.8 all-gather.42
  558.4 46.7 all-gather.44
  607.4 123.0 all-gather.46
  732.2 209.2 all-gather.48
  973.2 58.7 reduce-scatter.16
  1318.4 93.7 reduce-scatter.14
  1414.6 159.1 reduce-scatter.12
  1690.5 325.7 reduce-scatter.10
  2018.7 317.1 reduce-scatter.20
  2338.1 307.2 reduce-scatter.18
  2649.0 57.6 all-reduce.46
  2711.9 286.6 all-reduce.48
where the time goes:
time: 3050 us; the launch traced here: 3020 us
  waiting for transfers between devices  939 us (31%)
  blocking collectives  891 us (29%)
  matrix products  588 us (19%)
  local copies, waits for them, and re-layouts  293 us (10%)
  starting transfers between devices  240 us (8%)
  other arithmetic  49.9 us (2%)
    unnamed x3, blocking collectives  873 us
    ppermute x48, waiting for transfers between devices, shifted_2(): return lax.ppermute(array, axis, pairs)  361 us
    psum x1, waiting for transfers between devices, body(): lax.psum((share_input, share_output, share_expand, share_reduce, share_ga...  255 us
    ppermute x48, starting transfers between devices, shifted_2(): return lax.ppermute(array, axis, pairs)  234 us
    dot_general x104, matrix products, dot_last(): lax.dot_general(left_op, right_op, (((1,), (1,)), ((), ())), preferred_el...  216 us
    dot_general x72, matrix products, dot_first(): lax.dot_general(left_op, right_op, (((0,), (0,)), ((), ())), preferred_el...  193 us
    all_gather x2, waiting for transfers between devices, body(): lax.all_gather(reduce_weight[layer_index], 'fsdp', axis=0, tiled=True)  151 us
    unnamed x276, local copies, waits for them, and re-layouts  128 us
  transfers between devices with their start and end apart: 66, of which 28 were waited for; matrix products, arithmetic and copies ran while one was open for 56% of the time, Pallas kernels for 0%

commit v1 on v0

v1 whole, which is shorter than its diff:
```python
import functools
import math

import jax
import jax.numpy as jnp
from jax import lax
from jax.experimental import pallas as pl
from jax.experimental.pallas import tpu as pltpu
from jax.sharding import Mesh
from jax.sharding import PartitionSpec as P

HEADS = 16
CORES = 2
LANES = 128
EPSILON = 1e-06
GELU_COEF = math.sqrt(2.0 / math.pi)
MASKED = -1e30
F32 = jnp.float32
BF16 = jnp.bfloat16


def up(n, to=LANES):
    return -(-n // to) * to


def norm_forward(values, norm_gain, norm_bias):
    centre = jnp.mean(values, axis=-1, keepdims=True)
    shifted = values - centre
    spread = jnp.mean(shifted * shifted, axis=-1, keepdims=True)
    inverse = lax.rsqrt(spread + EPSILON)
    scaled = shifted * inverse
    return (scaled * norm_gain + norm_bias, scaled, inverse)


def norm_backward(upstream, scaled, inverse, norm_gain):
    weighted = upstream * norm_gain
    mean_one = jnp.mean(weighted, axis=-1, keepdims=True)
    mean_two = jnp.mean(weighted * scaled, axis=-1, keepdims=True)
    result = inverse * (weighted - mean_one - scaled * mean_two)
    return (result, jnp.sum(upstream * scaled, axis=0), jnp.sum(upstream, axis=0))


def gelu_tanh(inputs):
    inside = GELU_COEF * (inputs + 0.044715 * inputs * inputs * inputs)
    return 0.5 * inputs * (1.0 + jnp.tanh(inside))


def gelu_slope(inputs):
    inside = GELU_COEF * (inputs + 0.044715 * inputs * inputs * inputs)
    tangent = jnp.tanh(inside)
    return 0.5 * (1.0 + tangent) + 0.5 * inputs * (1.0 - tangent * tangent) * GELU_COEF * (
        1.0 + 3.0 * 0.044715 * inputs * inputs
    )


def dot(left_op, right_op):
    return jnp.dot(left_op, right_op, preferred_element_type=F32)


def dot_first(left_op, right_op):
    return lax.dot_general(
        left_op, right_op, (((0,), (0,)), ((), ())), preferred_element_type=F32
    )


def dot_last(left_op, right_op):
    return lax.dot_general(
        left_op, right_op, (((1,), (1,)), ((), ())), preferred_element_type=F32
    )


def attend_kernel(heads, scale, counts, pairs, q_ref, k_ref, v_ref, qid_ref, kid_ref,
                  out_ref, low_ref, log_ref, high, total, acc):
    here = pl.program_id(0)
    span = q_ref.shape[0]
    high[...] = jnp.full_like(high, MASKED)
    total[...] = jnp.zeros_like(total)
    acc[...] = jnp.zeros_like(acc)

    def step(n, carry):
        there = pairs[here, n]
        rows = pl.ds(pl.multiple_of(there * span, span), span)
        allowed = kid_ref[rows, :] == qid_ref[0]
        for h in range(heads):
            lanes = slice(h * LANES, (h + 1) * LANES)
            scores = dot_last(k_ref[rows, lanes], q_ref[:, lanes]) * scale
            scores = jnp.where(allowed, scores, MASKED)
            old = high[h]
            new = jnp.maximum(old, jnp.max(scores, axis=0, keepdims=True))
            kept = jnp.exp(old - new)
            weights = jnp.exp(scores - new)
            high[h] = new
            total[h] = total[h] * kept + jnp.sum(weights, axis=0, keepdims=True)
            acc[h] = acc[h] * kept + dot_first(v_ref[rows, lanes], weights.astype(BF16))
        return carry

    lax.fori_loop(0, counts[here], step, 0)
    for h in range(heads):
        lanes = slice(h * LANES, (h + 1) * LANES)
        result = (acc[h] / total[h]).T
        out_ref[:, lanes] = result
        low_ref[:, lanes] = result.astype(BF16)
        log_ref[0, h : h + 1, :] = high[h] + jnp.log(total[h])


def attend(projected, ids_column, ids_rows, counts, pairs, heads, scale):
    tokens = projected.shape[0]
    spans, span = ids_rows.shape[0], ids_rows.shape[2]
    wide = heads * LANES
    return pl.pallas_call(
        functools.partial(attend_kernel, heads, scale),
        grid_spec=pltpu.PrefetchScalarGridSpec(
            num_scalar_prefetch=2,
            grid=(spans,),
            in_specs=[
                pl.BlockSpec((span, wide), lambda i, *_: (i, 0)),
                pl.BlockSpec((tokens, wide), lambda i, *_: (0, 1)),
                pl.BlockSpec((tokens, wide), lambda i, *_: (0, 2)),
                pl.BlockSpec((1, 1, span), lambda i, *_: (i, 0, 0)),
                pl.BlockSpec((tokens, 1), lambda i, *_: (0, 0)),
            ],
            out_specs=[
                pl.BlockSpec((span, wide), lambda i, *_: (i, 0)),
                pl.BlockSpec((span, wide), lambda i, *_: (i, 0)),
                pl.BlockSpec((1, heads, span), lambda i, *_: (i, 0, 0)),
            ],
            scratch_shapes=[
                pltpu.VMEM((heads, 1, span), F32),
                pltpu.VMEM((heads, 1, span), F32),
                pltpu.VMEM((heads, LANES, span), F32),
            ],
        ),
        out_shape=[
            jax.ShapeDtypeStruct((tokens, wide), F32),
            jax.ShapeDtypeStruct((tokens, wide), BF16),
            jax.ShapeDtypeStruct((spans, heads, span), F32),
        ],
        cost_estimate=pl.CostEstimate(
            flops=2 * tokens * tokens * wide, bytes_accessed=12 * tokens * wide,
            transcendentals=tokens * tokens * heads // 2),
        name="attend",
    )(counts, pairs, projected, projected, projected, ids_rows, ids_column)


def attend_back_kernel(heads, scale, counts, pairs, q_ref, k_ref, v_ref, up_ref, out_ref, kid_ref,
                       qid_ref, log_ref, grad_ref, sums_ref, grad_q, grad_k, grad_v, dots):
    here = pl.program_id(0)
    span = k_ref.shape[0]
    wide = heads * LANES

    @pl.when(here == 0)
    def _():
        grad_q[...] = jnp.zeros_like(grad_q)
        sums_ref[...] = jnp.zeros_like(sums_ref)
        for i in range(dots.shape[0]):
            rows = slice(i * span, (i + 1) * span)
            for h in range(heads):
                lanes = slice(h * LANES, (h + 1) * LANES)
                product = up_ref[rows, lanes].astype(F32) * out_ref[rows, lanes]
                dots[i, h : h + 1, :] = jnp.sum(product.T, axis=0, keepdims=True)

    grad_k[...] = jnp.zeros_like(grad_k)
    grad_v[...] = jnp.zeros_like(grad_v)

    def step(n, carry):
        there = pairs[here, n]
        rows = pl.ds(pl.multiple_of(there * span, span), span)
        allowed = kid_ref[...] == qid_ref[there]
        for h in range(heads):
            lanes = slice(h * LANES, (h + 1) * LANES)
            queries = q_ref[rows, lanes]
            upstream = up_ref[rows, lanes]
            scores = dot_last(k_ref[:, lanes], queries) * scale
            scores = jnp.where(allowed, scores - log_ref[there, h : h + 1, :], MASKED)
            weights = jnp.exp(scores)
            slope = dot_last(v_ref[:, lanes], upstream) - dots[there, h : h + 1, :]
            slope = (weights * slope * scale).astype(BF16)
            grad_v[:, lanes] += dot(weights.astype(BF16), upstream)
            grad_k[:, lanes] += dot(slope, queries)
            grad_q[rows, lanes] += dot_first(slope, k_ref[:, lanes])
        return carry

    lax.fori_loop(0, counts[here], step, 0)
    mine = pl.ds(pl.multiple_of(here * span, span), span)
    grad_ref[mine, wide : 2 * wide] = grad_k[...].astype(BF16)
    grad_ref[mine, 2 * wide :] = grad_v[...].astype(BF16)
    sums_ref[1:2, :] += jnp.sum(grad_v[...], axis=0, keepdims=True)

    @pl.when(here == pl.num_programs(0) - 1)
    def _():
        grad_ref[:, :wide] = grad_q[...].astype(BF16)
        sums_ref[0:1, :] = jnp.sum(grad_q[...], axis=0, keepdims=True)


def attend_back(projected, upstream, attended, ids_column, ids_rows, log_rows, counts, pairs,
                heads, scale):
    tokens = projected.shape[0]
    spans, span = ids_rows.shape[0], ids_rows.shape[2]
    wide = heads * LANES
    return pl.pallas_call(
        functools.partial(attend_back_kernel, heads, scale),
        grid_spec=pltpu.PrefetchScalarGridSpec(
            num_scalar_prefetch=2,
            grid=(spans,),
            in_specs=[
                pl.BlockSpec((tokens, wide), lambda i, *_: (0, 0)),
                pl.BlockSpec((span, wide), lambda i, *_: (i, 1)),
                pl.BlockSpec((span, wide), lambda i, *_: (i, 2)),
                pl.BlockSpec((tokens, wide), lambda i, *_: (0, 0)),
                pl.BlockSpec((tokens, wide), lambda i, *_: (0, 0)),
                pl.BlockSpec((span, 1), lambda i, *_: (i, 0)),
                pl.BlockSpec((spans, 1, span), lambda i, *_: (0, 0, 0)),
                pl.BlockSpec((spans, heads, span), lambda i, *_: (0, 0, 0)),
            ],
            out_specs=[
                pl.BlockSpec((tokens, 3 * wide), lambda i, *_: (0, 0)),
                pl.BlockSpec((2, wide), lambda i, *_: (0, 0)),
            ],
            scratch_shapes=[
                pltpu.VMEM((tokens, wide), F32),
                pltpu.VMEM((span, wide), F32),
                pltpu.VMEM((span, wide), F32),
                pltpu.VMEM((spans, heads, span), F32),
            ],
        ),
        out_shape=[
            jax.ShapeDtypeStruct((tokens, 3 * wide), BF16),
            jax.ShapeDtypeStruct((2, wide), F32),
        ],
        cost_estimate=pl.CostEstimate(
            flops=5 * tokens * tokens * wide, bytes_accessed=16 * tokens * wide,
            transcendentals=tokens * tokens * heads // 2),
        name="attend_back",
    )(counts, pairs, projected, projected, projected, upstream, attended, ids_column,
      ids_rows, log_rows)


def body(
    reps,
    patches,
    cotangent,
    image_ids,
    input_weight,
    output_weight,
    expand_weight,
    reduce_weight,
    first_gain,
    first_shift,
    query_bias,
    value_bias,
    output_bias,
    second_gain,
    second_shift,
    expand_bias,
    reduce_bias,
):
    layers, own, _ = input_weight.shape
    span, width = patches.shape
    shards = reps * CORES
    tokens = span * shards
    own_ff = reduce_weight.shape[1]
    wide_ff = up(own_ff)
    heads = HEADS // shards
    head_dim = width // HEADS
    scale = 1.0 / math.sqrt(head_dim)
    wide = heads * LANES
    bits = reps.bit_length() - 1
    rep = lax.axis_index("rep")
    line = lax.axis_index("line")
    core = lax.axis_index("core")
    rank = rep * CORES + core
    every = ("rep", "line", "core")

    def ranked(r, z, c):
        return (r * reps + z) * CORES + c

    places = [(r, z, c) for r in range(reps) for z in range(reps) for c in range(CORES)]
    turned = [(ranked(r, z, c), ranked(r ^ z, r, c)) for r, z, c in places]
    turned_back = [(there, here) for here, there in turned]
    mates = [(ranked(r, z, c), ranked(r, z, 1 - c)) for r, z, c in places]

    def flip(step, c):
        return 1 << (step if c == 0 else bits - 1 - step)

    hops = [
        [(ranked(r, z, c), ranked(r ^ flip(step, c), z, c)) for r, z, c in places]
        for step in range(bits)
    ]

    line_hops = [
        [(ranked(r, z, c), ranked(r, z ^ (1 << step), c)) for r, z, c in places]
        for step in range(bits)
    ]
    rep_hops = [
        [(ranked(r, z, c), ranked(r ^ (1 << step), z, c)) for r, z, c in places]
        for step in range(bits)
    ]

    def relocate(array):
        return lax.ppermute(array, every, turned)

    def put_back(array):
        return lax.ppermute(array, every, turned_back)

    def swap(array):
        return lax.ppermute(array, every, mates)

    def after(array, other):
        return array + (other[(0,) * other.ndim] * 0).astype(array.dtype)

    def gather(array):
        for step in range(bits):
            array = jnp.concatenate([array, lax.ppermute(array, every, hops[step])])
        return array, swap(array)

    def scatter(pair, multiply):
        got = swap(multiply(pair[1]).astype(BF16))
        held = multiply(pair[0]) + got.astype(F32)
        for step in range(bits - 1, -1, -1):
            half = held.shape[0] // 2
            got = lax.ppermute(held[half:].astype(BF16), every, hops[step])
            held = held[:half] + got.astype(F32)
        return held

    def mirrored(j):
        return sum(((j >> b) & 1) << (bits - 1 - b) for b in range(bits))

    def spans_of(c):
        return [(jnp.where(c == 0, rep ^ j, rep ^ mirrored(j)) ^ line) * CORES + c
                for j in range(reps)]

    def collect(block, twist):
        block = block[None]
        for step in range(bits):
            block = jnp.concatenate([block, lax.ppermute(block, every, hops[step])])
        parts = []
        for a in range(reps):
            wanted = a ^ rep ^ twist
            part = block[0]
            for j in range(1, reps):
                at = jnp.where(core == 0, j, mirrored(j))
                part = jnp.where(wanted == at, block[j], part)
            parts.append(part)
        return parts

    order = jnp.stack(spans_of(core) + spans_of(1 - core))

    small = jnp.concatenate(
        [first_gain, first_shift, query_bias, value_bias, output_bias, second_gain,
         second_shift, reduce_bias, expand_bias], axis=1)
    small = lax.all_gather(small, ("line", "core"), axis=0, tiled=False)
    mine = lax.dynamic_index_in_dim(small, rank, 0, keepdims=False)
    normed = norm_forward(
        patches, small[:, 0, :own].reshape(width).astype(F32),
        small[:, 0, own : 2 * own].reshape(width).astype(F32))[0]
    normed = relocate(normed.astype(BF16))
    stream = relocate(after(patches, normed))
    ids = relocate(image_ids + (small[0, 0, 0] * 0).astype(jnp.int32))[0]
    ids = jnp.take(ids.reshape(shards, span), order, axis=0)
    ids_rows = ids.reshape(shards, 1, span)
    ids_column = ids.reshape(tokens, 1)
    first, last = ids[:, 0], ids[:, -1]
    meets = (first[:, None] <= last[None, :]) & (first[None, :] <= last[:, None])
    counts = jnp.sum(meets, axis=1, dtype=jnp.int32)
    before = jnp.arange(shards)[:, None] < jnp.arange(shards)[None, :]
    place = jnp.sum(meets[:, :, None] & before[None], axis=1, dtype=jnp.int32)
    chosen = meets[:, :, None] & (place[:, :, None] == jnp.arange(shards))
    pairs = jnp.sum(
        jnp.where(chosen, jnp.arange(shards, dtype=jnp.int32)[None, :, None], 0), axis=1,
        dtype=jnp.int32)

    def whole(index, layer):
        return small[:, layer, index * own : (index + 1) * own].reshape(width).astype(F32)

    def my_part(index, layer):
        return mine[layer, index * own : (index + 1) * own].astype(F32)

    def pad_heads(array):
        array = array.reshape(array.shape[:-1] + (heads, head_dim))
        array = jnp.pad(array, [(0, 0)] * (array.ndim - 1) + [(0, LANES - head_dim)])
        return array.reshape(array.shape[:-2] + (wide,))

    def cut_heads(array):
        array = array.reshape(array.shape[:-1] + (heads, LANES))[..., :head_dim]
        return array.reshape(array.shape[:-2] + (heads * head_dim,))

    start_ff = up(3 * own)

    own_up, own_ff_up = up(own, 16 * reps), up(own_ff, 16 * reps)

    def fetch_columns(of, other):
        kept, got = after(of(core), other), swap(after(of(1 - core), other))
        rows = jnp.where(core == 0, jnp.stack([kept, got]), jnp.stack([got, kept]))
        return lax.all_gather(rows.reshape(CORES * own, -1), "line", axis=0, tiled=True)

    def fetch_input(layer, other):
        def of(c):
            at = rep * CORES + c
            parts = [
                lax.dynamic_slice_in_dim(input_weight[layer], part * width + at * own, own, 1)
                for part in range(3)]
            parts.append(jnp.zeros((own, start_ff - 3 * own), BF16))
            return jnp.concatenate(parts, axis=1)

        return fetch_columns(of, other)

    def fetch_expand(layer, other):
        def of(c):
            return lax.dynamic_slice_in_dim(
                expand_weight[layer], (rep * CORES + c) * own_ff, own_ff, 1)

        return fetch_columns(of, other)

    def fetch_rows(layer, other):
        def piece(matrix, padded):
            matrix = jnp.pad(matrix, ((0, padded - matrix.shape[0]), (0, 0)))
            return lax.dynamic_slice_in_dim(
                matrix, (rep ^ line) * (padded // reps), padded // reps, 0)

        rows = jnp.concatenate(
            [piece(output_weight[layer], own_up), piece(reduce_weight[layer], own_ff_up)])
        return lax.all_gather(put_back(after(rows, other)), "line", axis=0, tiled=False)

    def unpack(fetched):
        columns, rows, expand_part = fetched
        input_part = jnp.concatenate(
            [pad_heads(columns[:, part * own : (part + 1) * own]) for part in range(3)], axis=1)
        expand_part = jnp.pad(expand_part, ((0, 0), (0, wide_ff - own_ff)))
        output_part = rows[:, : own_up // reps].reshape(own_up, width)[:own]
        output_part = jnp.pad(
            output_part.reshape(heads, head_dim, width), ((0, 0), (0, LANES - head_dim), (0, 0)))
        reduce_part = rows[:, own_up // reps :].reshape(own_ff_up, width)
        reduce_part = jnp.pad(reduce_part, ((0, wide_ff - own_ff_up), (0, 0)))
        return input_part, output_part.reshape(wide, width), expand_part, reduce_part

    def spread_columns(grad):
        return lax.psum_scatter(grad.astype(BF16), "line", scatter_dimension=0, tiled=True)

    def sides(grad):
        grad = grad.reshape(CORES, own, -1)
        kept = lax.dynamic_index_in_dim(grad, core, 0, keepdims=False)
        got = swap(lax.dynamic_index_in_dim(grad, 1 - core, 0, keepdims=False))
        return jnp.where(core == 0, jnp.stack([kept, got]), jnp.stack([got, kept]))

    def every_rep(block):
        return list(lax.all_gather(block, "rep", axis=0, tiled=False))

    def in_order(blocks):
        for bit in range(bits):
            turn = (line >> bit) & 1 == 1
            blocks = [jnp.where(turn, blocks[a ^ (1 << bit)], blocks[a]) for a in range(reps)]
        return blocks

    def join_input(parts):
        parts = [part[c].astype(F32) for part in parts for c in range(CORES)]
        return jnp.concatenate(
            [part[:, k * own : (k + 1) * own] for k in range(3) for part in parts], axis=1)

    def join_expand(parts):
        return jnp.concatenate(
            [part[c].astype(F32) for part in parts for c in range(CORES)], axis=1)

    def spread_rows(grad):
        rows = grad.shape[0]
        padded = jnp.pad(grad.astype(BF16), ((0, up(rows, 16 * reps) - rows), (0, 0)))
        return lax.psum_scatter(padded, "line", scatter_dimension=0, tiled=True)

    def join_rows(parts, rows):
        return jnp.concatenate(parts)[:rows].astype(F32)

    def both(function, *pairs_of):
        return tuple(function(*each) for each in zip(*pairs_of))

    def summed(left, right):
        return dot_first(left[0], right[0]) + dot_first(left[1], right[1])

    stored = []
    weights = []
    ahead_input = fetch_input(0, small)
    for layer in range(layers):
        gain_one, shift_one = whole(0, layer), whole(1, layer)
        again, scaled_one, inverse_one = norm_forward(stream, gain_one, shift_one)
        normed_all = gather(normed if layer == 0 else again.astype(BF16))
        if layer == 0:
            ahead = (ahead_input, fetch_rows(0, normed_all[0]), fetch_expand(0, normed_all[0]))
        weights.append(unpack(ahead))
        input_part, output_part, expand_part, reduce_part = weights[layer]
        bias = jnp.concatenate(
            [pad_heads(my_part(2, layer)), jnp.zeros((wide,), F32),
             pad_heads(my_part(3, layer))])
        projected = jnp.concatenate(
            both(lambda a: (dot(a, input_part) + bias).astype(BF16), normed_all))
        attended, attended_low, log_sum = attend(
            projected, ids_column, ids_rows, counts, pairs, heads, scale)
        if layer + 1 < layers:
            ahead = (fetch_input(layer + 1, attended_low), fetch_rows(layer + 1, attended_low),
                     fetch_expand(layer + 1, attended_low))
        halves = (attended_low[: tokens // 2], attended_low[tokens // 2 :])
        middle = (stream + scatter(halves, lambda a: dot(a, output_part))
                  + whole(4, layer))
        gain_two, shift_two = whole(5, layer), whole(6, layer)
        normed_two, scaled_two, inverse_two = norm_forward(middle, gain_two, shift_two)
        normed_two_all = gather(normed_two.astype(BF16))
        expand_bias_part = jnp.pad(mine[layer, 8 * own :], (0, wide_ff - own_ff)).astype(F32)
        if layer == max(layers - 2, 0):
            upstream = relocate(after(cotangent, normed_two_all[0]))
        hidden_pre = both(lambda a: dot(a, expand_part) + expand_bias_part, normed_two_all)
        hidden = both(lambda a: gelu_tanh(a).astype(BF16), hidden_pre)
        stream = (middle + scatter(hidden, lambda a: dot(a, reduce_part))
                  + whole(7, layer))
        stored.append(
            (gain_one, scaled_one, inverse_one, normed_all, projected, attended, halves,
             log_sum, gain_two, scaled_two, inverse_two, normed_two_all, hidden_pre, hidden))

    encoded = put_back(stream.astype(BF16)).astype(F32)
    grads = [None] * layers
    spreads = [None] * layers
    packed = [None] * layers
    here = (jnp.arange(shards) == rank).astype(F32)[:, None]
    for layer in range(layers - 1, -1, -1):
        input_part, output_part, expand_part, reduce_part = weights[layer]
        (gain_one, scaled_one, inverse_one, normed_all, projected, attended, halves,
         log_sum, gain_two, scaled_two, inverse_two, normed_two_all, hidden_pre, hidden,
         ) = stored[layer]
        upstream_low = upstream.astype(BF16)
        if layer + 1 == layers:
            upstream_low = after(upstream_low, hidden[0])
        upstream_all = gather(upstream_low)
        grad_reduce_bias = jnp.sum(upstream, axis=0)
        grad_pre = both(
            lambda u, h: dot_last(u, reduce_part) * gelu_slope(h), upstream_all, hidden_pre)
        grad_pre_low = both(lambda a: a.astype(BF16), grad_pre)
        grad_expand_bias = sum(both(lambda a: jnp.sum(a, axis=0)[:own_ff], grad_pre))
        grad_normed_two = scatter(grad_pre_low, lambda a: dot_last(a, expand_part))
        grad_reduce = summed(hidden, upstream_all)[:own_ff]
        grad_expand = summed(normed_two_all, grad_pre_low)[:, :own_ff]
        part_two, grad_gain_two, grad_shift_two = norm_backward(
            grad_normed_two, scaled_two, inverse_two, gain_two)
        grad_middle = upstream + part_two
        grad_middle_all = gather(grad_middle.astype(BF16))
        grad_output_bias = jnp.sum(grad_middle, axis=0)
        grad_attended = jnp.concatenate(
            both(lambda a: dot_last(a, output_part).astype(BF16), grad_middle_all))
        grad_projected, bias_sums = attend_back(
            projected, grad_attended, attended, ids_column, ids_rows, log_sum, counts, pairs,
            heads, scale)
        grad_projected = (grad_projected[: tokens // 2], grad_projected[tokens // 2 :])
        grad_normed = scatter(grad_projected, lambda a: dot_last(a, input_part))
        grad_output = summed(halves, grad_middle_all)
        grad_output = grad_output.reshape(heads, LANES, width)[:, :head_dim]
        grad_output = grad_output.reshape(own, width)
        grad_input = summed(normed_all, grad_projected)
        grad_input = jnp.concatenate(
            [cut_heads(grad_input[:, part * wide : (part + 1) * wide]) for part in range(3)],
            axis=1)
        part_one, grad_gain_one, grad_shift_one = norm_backward(
            grad_normed, scaled_one, inverse_one, gain_one)
        upstream = grad_middle + part_one
        mlp_spread = (spread_columns(grad_expand), spread_rows(grad_reduce))
        attention_spread = (spread_columns(grad_input), spread_rows(grad_output))
        spreads[layer] = (mlp_spread, attention_spread)
        if layer + 1 < layers:
            (late_expand, late_reduce), (late_input, late_output) = spreads[layer + 1]
            late = jnp.concatenate([late_input, late_expand], axis=1)
            parts = every_rep(sides(after(late, grad_middle_all[0])))
            late = jnp.concatenate([late_output, late_reduce])
            blocks = every_rep(relocate(after(late, grad_middle_all[0])))
            blocks = in_order(blocks)
            cut_at = late_output.shape[0]
            grads[layer + 1] = (
                join_input([part[:, :, : 3 * own] for part in parts]),
                join_rows([block[:cut_at] for block in blocks], own),
                join_expand([part[:, :, 3 * own :] for part in parts]),
                join_rows([block[cut_at:] for block in blocks], own_ff))

        def cut(vector):
            return vector.reshape(shards, -1)

        sums = jnp.concatenate(
            [cut(grad_gain_one), cut(grad_shift_one), here * cut_heads(bias_sums[0]),
             here * cut_heads(bias_sums[1]), cut(grad_output_bias), cut(grad_gain_two),
             cut(grad_shift_two), cut(grad_reduce_bias), here * grad_expand_bias], axis=1)
        packed[layer] = sums

    (last_expand, last_reduce), (last_input, last_output) = spreads[0]
    grads[0] = (
        join_input(collect(sides(last_input), 0)),
        join_rows(collect(relocate(last_output), line), own),
        join_expand(every_rep(sides(after(last_expand, grad_attended)))),
        join_rows(in_order(every_rep(relocate(after(last_reduce, grad_attended)))), own_ff))
    patch_grad = put_back(upstream.astype(BF16)).astype(F32)
    sums = jnp.stack(packed)
    for hop in [mates] + rep_hops + line_hops:
        sums = sums + lax.ppermute(sums, every, hop)
    sums = lax.dynamic_index_in_dim(sums, line * CORES + core, 1, keepdims=False)
    vectors = [sums[:, index * own : (index + 1) * own] for index in range(8)]
    vectors.append(sums[:, 8 * own :])
    stacked = [
        jnp.stack([grads[layer][member] for layer in range(layers)]) for member in range(4)]
    return (
        encoded, patch_grad, stacked[0], stacked[1], stacked[2], stacked[3],
        vectors[0], vectors[1], vectors[2], vectors[3], vectors[4], vectors[5], vectors[6],
        vectors[8], vectors[7],
    )


def solution(mesh):
    reps, shards = mesh.shape["rep"], mesh.shape["fsdp"]
    assert shards == reps * CORES and reps & (reps - 1) == 0 and HEADS % shards == 0
    own = ("line", "core")
    split = Mesh(mesh.devices.reshape(reps, reps, CORES), ("rep", "line", "core"))
    tokens = P(("rep",) + own, None)
    matrix, vector = P(None, own, None), P(None, own)
    return jax.shard_map(
        functools.partial(body, reps),
        mesh=split,
        in_specs=(tokens, tokens, P("rep", None)) + (matrix,) * 4 + (vector,) * 9,
        out_specs=(tokens, tokens) + (matrix,) * 4 + (vector,) * 9,
        check_vma=False,
    )
```

time: 3050 us -> 1500 us (0.49)
  the two profiles are of different devices: /device:TPU:0 before, /device:TPU:28 now
where the time goes in v1:
time: 1500 us; the launch traced here: 1490 us
  waiting for transfers between devices  746 us (50%)
  starting transfers between devices  169 us (11%)
  local copies, waits for them, and re-layouts  164 us (11%)
  matrix products  146 us (10%)
  Pallas kernels  115 us (8%)
  other arithmetic  113 us (8%)
  between operations  22.5 us (2%)
    ppermute x16, waiting for transfers between devices, scatter(): got = lax.ppermute(held[half:].astype(BF16), every, hops[step])  151 us
    ppermute x16, waiting for transfers between devices, gather(): array = jnp.concatenate([array, lax.ppermute(array, every, hops[step])])  134 us
    ppermute x7, waiting for transfers between devices, relocate(): return lax.ppermute(array, every, turned)  100 us
    all_gather x4, waiting for transfers between devices, fetch_columns(): lax.all_gather(rows.reshape(CORES * own, -1), 'line', axis=0, tiled=True)  80.4 us
    ppermute x16, starting transfers between devices, gather(): array = jnp.concatenate([array, lax.ppermute(array, every, hops[step])])  76.4 us
    ppermute x4, waiting for transfers between devices, put_back(): return lax.ppermute(array, every, turned_back)  71.5 us
    all_gather x4, waiting for transfers between devices, every_rep(): return list(lax.all_gather(block, 'rep', axis=0, tiled=False))  68.8 us
    pallas_call x2, Pallas kernels, attend_back(): pl.pallas_call(functools.partial(attend_back_kernel, heads, scale), grid_...  62.6 us
  transfers between devices with their start and end apart: 93, of which 63 were waited for; matrix products, arithmetic and copies ran while one was open for 22% of the time, Pallas kernels for 2%

profile of v1, /device:TPU:28, one launch (start us, length us, event | category | flops | bytes accessed | tf_op | source)
XLA Modules:
  0.0 1490.5 jit_solution(8903552470721457501)
XLA Ops:
  8.2 14.1 all-gather.5
  75.7 12.6 collective-permute-start.4
  94.8 22.6 %collective-permute-done.7 = bf16[192,1152]{1,0:T(8,128)(2,1)S(1)} collective-permute-done((bf16[192,1152]{1,0:T(8,128)(2,1)}, bf16[192,1152]{1,0:T(8,128)(2,1)S(1)}, u32[]{:S(2)}, u32[]{:S(2)}) %collective-permute-start.7) | collective-permute-done | bytes 442400 | tf_op jit(solution)/shard_map/ppermute | solution.py:303
  134.5 31.4 %all-gather.29.cloned.1.call-done = bf16[768,1152]{1,0:T(8,128)(2,1)} async-done(((bf16[192,1152]{1,0:T(8,128)(2,1)}), bf16[768,1152]{1,0:T(8,128)(2,1)}) %all-gather.29.cloned.1.call-update) | async-done | bytes 1769488 | tf_op jit(solution)/shard_map/all_gather | solution.py:422
  173.5 26.4 %attend.2 = (f32[2048,256]{1,0:T(8,128)}, bf16[2048,256]{1,0:T(8,128)(2,1)}, f32[8,2,256]{2,1,0:T(2,128)}) custom-call(s32[8]{0:T(128)} %convert_reduce_fusion.1.counts, s32[8,8]{1,0:T(8,128)} %select_reduce_fusion.pairs, bf16[2048,768]{1,0:T(8,128)(2,1)} %pad_maximum_fusion.1.q_ref.k_ref.v_ref, bf16[2048,768]{1,0:T(8,128)(2,1)} %pad_maximum_fusion.1.q_ref.k_ref.v_ref, ...), custom_call_target="tpu_custom_call" | custom-call | flops 2147483648 | bytes 6291456 | tf_op jit(solution)/shard_map/attend/pallas_call | solution.py:110
  215.5 16.5 %collective-permute-done.9 = bf16[512,1152]{1,0:T(8,128)(2,1)} collective-permute-done((bf16[512,1152]{1,0:T(8,128)(2,1)S(1)}, bf16[512,1152]{1,0:T(8,128)(2,1)}, u32[]{:S(2)}, u32[]{:S(2)}) %collective-permute-start.9) | collective-permute-done | bytes 1179680 | tf_op jit(solution)/shard_map/ppermute | solution.py:321
  239.3 28.8 %collective-permute-done.1 = f32[256,1152]{1,0:T(8,128)S(1)} collective-permute-done((f32[256,1152]{1,0:T(8,128)S(1)}, f32[256,1152]{1,0:T(8,128)S(1)}, u32[]{:S(2)}, u32[]{:S(2)}) %collective-permute-start.1) | collective-permute-done | bytes 1179680 | tf_op jit(solution)/shard_map/ppermute | solution.py:300
  304.9 14.2 collective-permute-done.12
  330.1 33.6 %all-gather.19.cloned.1.call-done = bf16[1152,538]{1,0:T(8,128)(2,1)} async-done(((bf16[288,538]{1,0:T(8,128)(2,1)}), bf16[1152,538]{1,0:T(8,128)(2,1)}) %all-gather.19.cloned.1.call-update) | async-done | bytes 1239568 | tf_op jit(solution)/shard_map/all_gather | solution.py:394
  380.0 15.7 %collective-permute-done.16 = bf16[512,1152]{1,0:T(8,128)(2,1)S(1)} collective-permute-done((bf16[512,1152]{1,0:T(8,128)(2,1)S(1)}, bf16[512,1152]{1,0:T(8,128)(2,1)S(1)}, u32[]{:S(2)}, u32[]{:S(2)}) %collective-permute-start.16) | collective-permute-done | bytes 1179680 | tf_op jit(solution)/shard_map/ppermute | solution.py:321
  425.8 19.0 %collective-permute-done.22 = bf16[192,1152]{1,0:T(8,128)(2,1)S(1)} collective-permute-done((bf16[192,1152]{1,0:T(8,128)(2,1)S(1)}, bf16[192,1152]{1,0:T(8,128)(2,1)S(1)}, u32[]{:S(2)}, u32[]{:S(2)}) %collective-permute-start.22) | collective-permute-done | bytes 442400 | tf_op jit(solution)/shard_map/ppermute | solution.py:303
  463.2 30.1 %all-gather.31.cloned.1.call-done = bf16[768,1152]{1,0:T(8,128)(2,1)} async-done(((bf16[192,1152]{1,0:T(8,128)(2,1)}), bf16[768,1152]{1,0:T(8,128)(2,1)}) %all-gather.31.cloned.1.call-update) | async-done | bytes 1769488 | tf_op jit(solution)/shard_map/all_gather | solution.py:422
  504.4 26.4 %attend.3 = (f32[2048,256]{1,0:T(8,128)}, bf16[2048,256]{1,0:T(8,128)(2,1)}, f32[8,2,256]{2,1,0:T(2,128)}) custom-call(s32[8]{0:T(128)} %convert_reduce_fusion.1.counts, s32[8,8]{1,0:T(8,128)} %select_reduce_fusion.pairs, bf16[2048,768]{1,0:T(8,128)(2,1)} %pad_maximum_fusion.2.q_ref.k_ref.v_ref, bf16[2048,768]{1,0:T(8,128)(2,1)} %pad_maximum_fusion.2.q_ref.k_ref.v_ref, ...), custom_call_target="tpu_custom_call" | custom-call | flops 2147483648 | bytes 6291456 | tf_op jit(solution)/shard_map/attend/pallas_call | solution.py:110
  539.0 15.6 %collective-permute-done.24 = bf16[512,1152]{1,0:T(8,128)(2,1)S(1)} collective-permute-done((bf16[512,1152]{1,0:T(8,128)(2,1)S(1)}, bf16[512,1152]{1,0:T(8,128)(2,1)S(1)}, u32[]{:S(2)}, u32[]{:S(2)}) %collective-permute-start.24) | collective-permute-done | bytes 1179680 | tf_op jit(solution)/shard_map/ppermute | solution.py:321
  590.2 46.8 %all-gather.23.cloned.1.call-done = bf16[1152,538]{1,0:T(8,128)(2,1)} async-done(((bf16[288,538]{1,0:T(8,128)(2,1)}), bf16[1152,538]{1,0:T(8,128)(2,1)}) %all-gather.23.cloned.1.call-update) | async-done | bytes 1239568 | tf_op jit(solution)/shard_map/all_gather | solution.py:394
  642.5 13.1 collective-permute-done.34
  656.9 14.5 collective-permute-start.35
  679.4 13.0 collective-permute-start.36
  694.1 12.5 collective-permute-done.36
  748.7 14.6 collective-permute-done.31
  790.5 14.2 collective-permute-done.42
  811.9 31.5 %attend_back.2 = (bf16[2048,768]{1,0:T(8,128)(2,1)}, f32[2,256]{1,0:T(2,128)}) custom-call(s32[8]{0:T(128)} %convert_reduce_fusion.1.counts, s32[8,8]{1,0:T(8,128)} %select_reduce_fusion.pairs, bf16[2048,768]{1,0:T(8,128)(2,1)} %pad_maximum_fusion.2.q_ref.k_ref.v_ref, bf16[2048,768]{1,0:T(8,128)(2,1)} %pad_maximum_fusion.2.q_ref.k_ref.v_ref, ...), custom_call_target="tpu_custom_call" | custom-call | flops 5368709120 | bytes 8388608 | tf_op jit(solution)/shard_map/attend_back/pallas_call | solution.py:200
  856.4 14.2 collective-permute-done.45
  895.5 14.2 collective-permute-done.48
  989.4 14.2 collective-permute-done.51
  1023.2 37.3 %collective-permute-done.67 = bf16[192,1152]{1,0:T(8,128)(2,1)S(1)} collective-permute-done((bf16[192,1152]{1,0:T(8,128)(2,1)S(1)}, bf16[192,1152]{1,0:T(8,128)(2,1)S(1)}, u32[]{:S(2)}, u32[]{:S(2)}) %collective-permute-start.67) | collective-permute-done | bytes 442400 | tf_op jit(solution)/shard_map/ppermute | solution.py:300
  1085.0 14.2 collective-permute-done.54
  1112.3 29.9 %collective-permute-done.33 = bf16[256,1152]{1,0:T(8,128)(2,1)S(1)} collective-permute-done((bf16[256,1152]{1,0:T(8,128)(2,1)}, bf16[256,1152]{1,0:T(8,128)(2,1)S(1)}, u32[]{:S(2)}, u32[]{:S(2)}) %collective-permute-start.33) | collective-permute-done | bytes 589856 | tf_op jit(solution)/shard_map/ppermute | solution.py:303
  1175.7 27.5 %all-gather.33.cloned.1.call-done = bf16[768,1152]{1,0:T(8,128)(2,1)} async-done(((bf16[192,1152]{1,0:T(8,128)(2,1)}), bf16[768,1152]{1,0:T(8,128)(2,1)}) %all-gather.33.cloned.1.call-update) | async-done | bytes 1769488 | tf_op jit(solution)/shard_map/all_gather | solution.py:446
  1207.0 35.8 %all-gather.25.cloned.1.call-done = bf16[4,2,144,970]{3,2,1,0:T(8,128)(2,1)} async-done(((bf16[1,2,144,970]{3,2,1,0:T(8,128)(2,1)}), bf16[4,2,144,970]{3,2,1,0:T(8,128)(2,1)}) %all-gather.25.cloned.1.call-update) | async-done | bytes 2234896 | tf_op jit(solution)/shard_map/all_gather | solution.py:446
  1293.7 31.0 %attend_back.3 = (bf16[2048,768]{1,0:T(8,128)(2,1)}, f32[2,256]{1,0:T(2,128)}) custom-call(s32[8]{0:T(128)} %convert_reduce_fusion.1.counts, s32[8,8]{1,0:T(8,128)} %select_reduce_fusion.pairs, bf16[2048,768]{1,0:T(8,128)(2,1)} %pad_maximum_fusion.1.q_ref.k_ref.v_ref, bf16[2048,768]{1,0:T(8,128)(2,1)} %pad_maximum_fusion.1.q_ref.k_ref.v_ref, ...), custom_call_target="tpu_custom_call" | custom-call | flops 5368709120 | bytes 8388608 | tf_op jit(solution)/shard_map/attend_back/pallas_call | solution.py:200
  1454.0 26.9 %collective-permute-done.74 = f32[2,8,1690]{2,0,1:T(2,128)S(1)} collective-permute-done((f32[2,8,1690]{2,0,1:T(2,128)S(1)}, f32[2,8,1690]{2,0,1:T(2,128)S(1)}, u32[]{:S(2)}, u32[]{:S(2)}) %collective-permute-start.74) | collective-permute-done | bytes 108192 | tf_op jit(solution)/shard_map/ppermute | solution.py:594
  (890 shorter events, 755.8 us)
Async XLA Ops:
  7.2 118.4 %all-gather.17.cloned.1.call-start = ((), (), s32[]{:S(2)}) async-start(), calls=%async_computation.8 | async-start | bytes 1474560 | tf_op jit(solution)/shard_map/all_gather | solution.py:394
  24.2 68.0 %collective-permute-start.2 = (s32[1,2048]{1,0:T(1,128)S(1)}, s32[1,2048]{1,0:T(1,128)S(1)}, u32[]{:S(2)}, u32[]{:S(2)}) collective-permute-start(s32[1,2048]{1,0:T(1,128)S(1)} %broadcast_add_fusion.4), channel_id=1, source_target_pairs={{0,0},{1,1},{2,8},{3,9},{4,16},{5,17},{6,24},{7,25},{8,10},{9,11},... | collective-permute-start | bytes 24584 | tf_op jit(solution)/shard_map/ppermute | solution.py:300
  65.3 100.7 %all-gather.29.cloned.1.call-start = ((), (), s32[]{:S(2)}) async-start(), calls=%async_computation.19 | async-start | bytes 2211840 | tf_op jit(solution)/shard_map/all_gather | solution.py:422
  75.7 44.7 %collective-permute-start.4 = (bf16[512,1152]{1,0:T(8,128)(2,1)}, bf16[512,1152]{1,0:T(8,128)(2,1)S(1)}, u32[]{:S(2)}, u32[]{:S(2)}) collective-permute-start(bf16[512,1152]{1,0:T(8,128)(2,1)} %pad_maximum_fusion.18), channel_id=1, source_target_pairs={{0,16},{1,9},{2,18},{3,11},{4,20},{5,13},{6,22},{7,15},{8,24},{9,1... | collective-permute-start | bytes 3538952 | tf_op jit(solution)/shard_map/ppermute | solution.py:313
  118.2 245.5 %all-gather.19.cloned.1.call-start = ((), (), s32[]{:S(2)}) async-start(), calls=%async_computation.9 | async-start | bytes 1843200 | tf_op jit(solution)/shard_map/all_gather | solution.py:394
  121.6 45.5 %collective-permute-start.6 = (bf16[1024,1152]{1,0:T(8,128)(2,1)}, bf16[1024,1152]{1,0:T(8,128)(2,1)}, u32[]{:S(2)}, u32[]{:S(2)}) collective-permute-start(bf16[1024,1152]{1,0:T(8,128)(2,1)} %constant_dynamic-update-slice_fusion), channel_id=1, source_target_pairs={{0,1},{1,0},{2,3},{3,2},{4,5},{5,4},{6,7},{7,6},{8,9},{9,8},{10,11... | collective-permute-start | bytes 7077896 | tf_op jit(solution)/shard_map/ppermute | solution.py:306
  210.3 57.8 %collective-permute-start.1 = (f32[256,1152]{1,0:T(8,128)S(1)}, f32[256,1152]{1,0:T(8,128)S(1)}, u32[]{:S(2)}, u32[]{:S(2)}) collective-permute-start(f32[256,1152]{1,0:T(8,128)S(1)} %broadcast_add_fusion.1), channel_id=1, source_target_pairs={{0,0},{1,1},{2,8},{3,9},{4,16},{5,17},{6,24},{7,25},{8,10},{9,11},... | collective-permute-start | bytes 3538952 | tf_op jit(solution)/shard_map/ppermute | solution.py:300
  235.7 44.2 %collective-permute-start.10 = (bf16[256,1152]{1,0:T(8,128)(2,1)S(1)}, bf16[256,1152]{1,0:T(8,128)(2,1)S(1)}, u32[]{:S(2)}, u32[]{:S(2)}) collective-permute-start(bf16[256,1152]{1,0:T(8,128)(2,1)S(1)} %slice.1612), channel_id=1, source_target_pairs={{0,8},{1,17},{2,10},{3,19},{4,12},{5,21},{6,14},{7,23},{8,0},{9,25... | collective-permute-start | bytes 1769480 | tf_op jit(solution)/shard_map/ppermute | solution.py:321
  320.9 42.9 %collective-permute-start.14 = (bf16[1024,1152]{1,0:T(8,128)(2,1)}, bf16[1024,1152]{1,0:T(8,128)(2,1)}, u32[]{:S(2)}, u32[]{:S(2)}) collective-permute-start(bf16[1024,1152]{1,0:T(8,128)(2,1)} %pad_maximum_fusion.3), channel_id=1, source_target_pairs={{0,1},{1,0},{2,3},{3,2},{4,5},{5,4},{6,7},{7,6},{8,9},{9,8},{10,11... | collective-permute-start | bytes 7077896 | tf_op jit(solution)/shard_map/ppermute | solution.py:306
  326.7 122.8 %all-gather.21.cloned.1.call-start = ((), (), s32[]{:S(2)}) async-start(), calls=%async_computation.10 | async-start | bytes 1474560 | tf_op jit(solution)/shard_map/all_gather | solution.py:394
  406.0 87.3 %all-gather.31.cloned.1.call-start = ((), (), s32[]{:S(2)}) async-start(), calls=%async_computation.20 | async-start | bytes 2211840 | tf_op jit(solution)/shard_map/all_gather | solution.py:422
  445.6 191.4 %all-gather.23.cloned.1.call-start = ((), (), s32[]{:S(2)}) async-start(), calls=%async_computation.11 | async-start | bytes 1843200 | tf_op jit(solution)/shard_map/all_gather | solution.py:394
  449.5 49.2 %collective-permute-start.21 = (bf16[1024,1152]{1,0:T(8,128)(2,1)}, bf16[1024,1152]{1,0:T(8,128)(2,1)}, u32[]{:S(2)}, u32[]{:S(2)}) collective-permute-start(bf16[1024,1152]{1,0:T(8,128)(2,1)} %pad_maximum_fusion.4), channel_id=1, source_target_pairs={{0,1},{1,0},{2,3},{3,2},{4,5},{5,4},{6,7},{7,6},{8,9},{9,8},{10,11... | collective-permute-start | bytes 7077896 | tf_op jit(solution)/shard_map/ppermute | solution.py:306
  570.9 448.4 %reduce-scatter.19.cloned.1.call-start = ((), (), s32[]{:S(2)}) async-start(), calls=%async_computation.15 | async-start | bytes 552960 | tf_op jit(solution)/shard_map/reduce_scatter | solution.py:466
  580.7 56.3 %collective-permute-start.27 = (bf16[512,1152]{1,0:T(8,128)(2,1)}, bf16[512,1152]{1,0:T(8,128)(2,1)}, u32[]{:S(2)}, u32[]{:S(2)}) collective-permute-start(bf16[512,1152]{1,0:T(8,128)(2,1)} %pad_maximum_fusion.21), channel_id=1, source_target_pairs={{0,16},{1,9},{2,18},{3,11},{4,20},{5,13},{6,22},{7,15},{8,24},{9,1... | collective-permute-start | bytes 3538952 | tf_op jit(solution)/shard_map/ppermute | solution.py:313
  584.8 70.8 %collective-permute-start.34 = (f32[256,1152]{1,0:T(8,128)}, f32[256,1152]{1,0:T(8,128)}, u32[]{:S(2)}, u32[]{:S(2)}) collective-permute-start(f32[256,1152]{1,0:T(8,128)} %broadcast_add_fusion), channel_id=1, source_target_pairs={{0,0},{1,1},{2,8},{3,9},{4,16},{5,17},{6,24},{7,25},{8,10},{9,11},... | collective-permute-start | bytes 3538952 | tf_op jit(solution)/shard_map/ppermute | solution.py:300
  922.2 97.1 %reduce-scatter.21.cloned.1.call-start = ((), (), s32[]{:S(2)}) async-start(), calls=%async_computation.16 | async-start | bytes 1658880 | tf_op jit(solution)/shard_map/reduce_scatter | solution.py:466
  932.8 128.5 %reduce-scatter.27.cloned.1.call-start = ((), (), s32[]{:S(2)}) async-start(), calls=%async_computation.24 | async-start | bytes 1843200 | tf_op jit(solution)/shard_map/reduce_scatter | solution.py:437
  942.8 118.6 %reduce-scatter.25.cloned.1.call-start = ((), (), s32[]{:S(2)}) async-start(), calls=%async_computation.23 | async-start | bytes 1474560 | tf_op jit(solution)/shard_map/reduce_scatter | solution.py:437
  953.2 150.1 %reduce-scatter.29.cloned.1.call-start = ((), (), s32[]{:S(2)}) async-start(), calls=%async_computation.25 | async-start | bytes 1843200 | tf_op jit(solution)/shard_map/reduce_scatter | solution.py:437
  979.9 173.9 %reduce-scatter.23.cloned.1.call-start = ((), (), s32[]{:S(2)}) async-start(), calls=%async_computation.18 | async-start | bytes 1658880 | tf_op jit(solution)/shard_map/reduce_scatter | solution.py:466
  989.3 213.9 %all-gather.33.cloned.1.call-start = ((), (), s32[]{:S(2)}) async-start(), calls=%async_computation.21 | async-start | bytes 2211840 | tf_op jit(solution)/shard_map/all_gather | solution.py:446
  1020.3 40.1 %collective-permute-start.67 = (bf16[192,1152]{1,0:T(8,128)(2,1)S(1)}, bf16[192,1152]{1,0:T(8,128)(2,1)S(1)}, u32[]{:S(2)}, u32[]{:S(2)}) collective-permute-start(bf16[192,1152]{1,0:T(8,128)(2,1)S(1)} %maximum_add_fusion.3), channel_id=1, source_target_pairs={{0,0},{1,1},{2,8},{3,9},{4,16},{5,17},{6,24},{7,25},{8,10},{9,11},... | collective-permute-start | bytes 1327112 | tf_op jit(solution)/shard_map/ppermute | solution.py:300
  1061.3 181.6 %all-gather.25.cloned.1.call-start = ((), (), s32[]{:S(2)}) async-start(), calls=%async_computation.13 | async-start | bytes 2949120 | tf_op jit(solution)/shard_map/all_gather | solution.py:446
  1065.4 209.8 %all-gather.27.cloned.1.call-start = ((), (), s32[]{:S(2)}) async-start(), calls=%async_computation.17 | async-start | bytes 1843200 | tf_op jit(solution)/shard_map/all_gather | solution.py:446
  1104.5 37.7 %collective-permute-start.33 = (bf16[256,1152]{1,0:T(8,128)(2,1)}, bf16[256,1152]{1,0:T(8,128)(2,1)S(1)}, u32[]{:S(2)}, u32[]{:S(2)}) collective-permute-start(bf16[256,1152]{1,0:T(8,128)(2,1)} %get-tuple-element.195), channel_id=1, source_target_pairs={{0,0},{1,1},{8,2},{9,3},{16,4},{17,5},{24,6},{25,7},{10,8},{11,9},... | collective-permute-start | bytes 1769480 | tf_op jit(solution)/shard_map/ppermute | solution.py:303
  1109.5 224.9 %all-gather.35.cloned.1.call-start = ((), (), s32[]{:S(2)}) async-start(), calls=%async_computation.22 | async-start | bytes 1658880 | tf_op jit(solution)/shard_map/all_gather | solution.py:446
  1172.7 112.7 %collective-permute-start.55 = (bf16[1024,1152]{1,0:T(8,128)(2,1)}, bf16[1024,1152]{1,0:T(8,128)(2,1)}, u32[]{:S(2)}, u32[]{:S(2)}) collective-permute-start(bf16[1024,1152]{1,0:T(8,128)(2,1)} %pad_maximum_fusion.9), channel_id=1, source_target_pairs={{0,1},{1,0},{2,3},{3,2},{4,5},{5,4},{6,7},{7,6},{8,9},{9,8},{10,11... | collective-permute-start | bytes 7077896 | tf_op jit(solution)/shard_map/ppermute | solution.py:306
  1175.7 166.7 %reduce-scatter.17.cloned.1.call-start = ((), (), s32[]{:S(2)}) async-start(), calls=%async_computation.14 | async-start | bytes 552960 | tf_op jit(solution)/shard_map/reduce_scatter | solution.py:466
  1293.4 77.6 %reduce-scatter.15.cloned.1.call-start = ((), (), s32[]{:S(2)}) async-start(), calls=%async_computation.12 | async-start | bytes 1474560 | tf_op jit(solution)/shard_map/reduce_scatter | solution.py:437
  1341.2 41.4 %collective-permute-start.56 = (bf16[1024,1152]{1,0:T(8,128)(2,1)}, bf16[1024,1152]{1,0:T(8,128)(2,1)}, u32[]{:S(2)}, u32[]{:S(2)}) collective-permute-start(bf16[1024,1152]{1,0:T(8,128)(2,1)} %convolution_convert_fusion), channel_id=1, source_target_pairs={{0,1},{1,0},{2,3},{3,2},{4,5},{5,4},{6,7},{7,6},{8,9},{9,8},{10,11... | collective-permute-start | bytes 7077896 | tf_op jit(solution)/shard_map/ppermute | solution.py:306
  1444.6 37.5 %collective-permute-start.59 = (bf16[256,1152]{1,0:T(8,128)(2,1)S(1)}, bf16[256,1152]{1,0:T(8,128)(2,1)S(1)}, u32[]{:S(2)}, u32[]{:S(2)}) collective-permute-start(bf16[256,1152]{1,0:T(8,128)(2,1)S(1)} %add_convert_fusion.4), channel_id=1, source_target_pairs={{0,0},{1,1},{8,2},{9,3},{16,4},{17,5},{24,6},{25,7},{10,8},{11,9},... | collective-permute-start | bytes 1769480 | tf_op jit(solution)/shard_map/ppermute | solution.py:303
  (234 other events, 3847.0 us)
Sparse Core Ops, SparseCore 0:
  65.4 57.2 all-gather.16
  124.8 41.0 all-gather.28
  326.9 36.8 all-gather.18
  406.1 42.0 all-gather.20
  449.7 43.6 all-gather.30
  571.0 65.9 all-gather.22
  922.3 20.2 reduce-scatter.18
  944.9 31.0 reduce-scatter.20
  978.8 32.6 reduce-scatter.26
  1013.7 42.1 reduce-scatter.24
  1058.2 45.0 reduce-scatter.28
  1105.5 48.3 reduce-scatter.22
  1155.7 47.4 all-gather.32
  1205.5 37.3 all-gather.24
  1245.1 30.0 all-gather.26
  1276.9 28.7 all-gather.34
  1308.4 18.1 reduce-scatter.16
  1334.5 30.8 reduce-scatter.14
